TPU v7x, 128 devices: a whole 4x4x4 slice. The times are simulated.
128 devices in a mesh: gx: 8 (over x, core), gy: 16 (over y, z).
Axes of the slice: x: 4, y: 4, z: 4, core: 2. Of those that a mesh axis runs over, the one named last changes fastest.
Arguments:
- wave_prev: float32 [256, 1024, 512], P('gx', 'gy'), may hold values from -6 to 6
- wave_now: float32 [256, 1024, 512], P('gx', 'gy'), may hold values from -6 to 6
- courant: float32 [256, 1024, 512], P('gx', 'gy'), may hold values from 0.02 to 0.18
- traces: bfloat16 [524288, 128], P(('gx', 'gy')), may hold values from -6 to 6
- pair_owner: int32 [524288, 1], P(('gx', 'gy')), may hold values from 0 to 127; in each aligned block of 4096 rows (0 to 4095, 4096 to 8191, ...) at most 64 rows name the same one
- pair_cell: int32 [524288], P(('gx', 'gy')), may hold values from 0 to 2047
- green_tiles: bfloat16 [131072, 2048], P(('gx', 'gy')), may hold values from -0.09375 to 0.09375
Outputs:
- wave_before: float32 [256, 1024, 512], P('gx', 'gy')
- wave_after: float32 [256, 1024, 512], P('gx', 'gy')
Inputs may be any that keep to these rules, and one draw needn't show every extreme that they name: `pair_owner`: within the rows of one device no owner is named by more than 64 rows, a bound that some block reaches.
All inputs are finite; a program needn't handle non-finite values.
Results may differ from a plain program's by a relative error of at most 0.00049.
Values may be sent and summed in bfloat16 or wider, within the bound.
A program may use at most 192 MiB of HBM per device.

v0:
```python
import jax
import jax.numpy as jnp
from jax import lax
from jax.sharding import PartitionSpec as P

STEPS = 4


stencil_center = -205.0 / 72.0
stencil_side = (8.0 / 5.0, -1.0 / 5.0, 8.0 / 315.0, -1.0 / 560.0)


def padded_2(block, sides, width):
    for axis, dim in sides:
        count = lax.axis_size(axis)
        forward = [(i, i + 1) for i in range(count - 1)]
        backward = [(target, source) for source, target in forward]
        low = lax.ppermute(
            lax.slice_in_dim(block, block.shape[dim] - width, None, axis=dim), axis, forward
        )
        high = lax.ppermute(lax.slice_in_dim(block, 0, width, axis=dim), axis, backward)
        block = jnp.concatenate([low, block, high], axis=dim)
    return block


def laplace_padded(padded, size_first, size_second, size_depth):
    middle = padded[4 : 4 + size_first, 4 : 4 + size_second, 4 : 4 + size_depth]
    result = 3.0 * stencil_center * middle
    for offset in range(1, 5):
        weight = stencil_side[offset - 1]
        beside_all = padded[
            4 + offset : 4 + offset + size_first, 4 : 4 + size_second, 4 : 4 + size_depth
        ]
        beside_all = (
            beside_all
            + padded[4 - offset : 4 - offset + size_first, 4 : 4 + size_second, 4 : 4 + size_depth]
        )
        beside_all = (
            beside_all
            + padded[4 : 4 + size_first, 4 + offset : 4 + offset + size_second, 4 : 4 + size_depth]
        )
        beside_all = (
            beside_all
            + padded[4 : 4 + size_first, 4 - offset : 4 - offset + size_second, 4 : 4 + size_depth]
        )
        beside_all = (
            beside_all
            + padded[4 : 4 + size_first, 4 : 4 + size_second, 4 + offset : 4 + offset + size_depth]
        )
        beside_all = (
            beside_all
            + padded[4 : 4 + size_first, 4 : 4 + size_second, 4 - offset : 4 - offset + size_depth]
        )
        result = result + weight * beside_all
    return result


def on_device(wave_prev, wave_now, courant, traces, pair_owner, pair_cell, green_tiles):
    slab_count = lax.axis_size("gx")
    block_count = lax.axis_size("gy")
    devices = slab_count * block_count
    row_count, samples = traces.shape
    size_first, size_second, size_depth = wave_now.shape
    cell_count = size_first * size_second
    capacity = 2 * row_count // devices
    target = pair_owner[:, 0]
    ordering = jnp.argsort(target, stable=True)
    sorted_target = target[ordering]
    owner_ids = jnp.arange(devices, dtype=jnp.int32)
    counts_per = jnp.sum((target[:, None] == owner_ids[None, :]).astype(jnp.int32), axis=0)
    starts_per = jnp.cumsum(counts_per) - counts_per
    matches = sorted_target[:, None] == owner_ids[None, :]
    first_row = jnp.sum(jnp.where(matches, starts_per[None, :], 0), axis=1)
    rank_within = jnp.arange(row_count, dtype=jnp.int32) - first_row
    slot_index = sorted_target * capacity + rank_within
    send_rows = (
        jnp.zeros((devices * capacity, samples), traces.dtype).at[slot_index].set(traces[ordering])
    )
    send_cells = jnp.zeros((devices * capacity,), jnp.int32).at[slot_index].set(pair_cell[ordering])
    got_rows, got_cells = (
        lax.all_to_all(
            send_rows.reshape(devices, capacity, samples),
            ("gx", "gy"),
            split_axis=0,
            concat_axis=0,
            tiled=True,
        ),
        lax.all_to_all(
            send_cells.reshape(devices, capacity),
            ("gx", "gy"),
            split_axis=0,
            concat_axis=0,
            tiled=True,
        ),
    )
    got_rows = got_rows.reshape(slab_count, block_count * capacity, samples)
    got_cells = got_cells.reshape(slab_count, block_count * capacity)
    slab_ids = jnp.arange(slab_count, dtype=jnp.int32)[:, None]
    segment = (got_cells * slab_count + slab_ids).reshape(-1)
    summed = jax.ops.segment_sum(
        got_rows.reshape(-1, samples).astype(jnp.float32),
        segment,
        num_segments=cell_count * slab_count,
    )
    gathered = summed.reshape(cell_count, slab_count * samples).astype(jnp.bfloat16)
    response = jnp.dot(gathered, green_tiles, preferred_element_type=jnp.float32)
    previous, current = (wave_prev, wave_now)
    for time_step in range(STEPS):
        source = response[:, time_step * size_depth : (time_step + 1) * size_depth]
        source = source.reshape(size_first, size_second, size_depth)
        padded = padded_2(current, (("gx", 0), ("gy", 1)), 4)
        padded = jnp.pad(padded, ((0, 0), (0, 0), (4, 4)))
        following = (
            2.0 * current
            - previous
            + courant * laplace_padded(padded, size_first, size_second, size_depth)
            + source
        )
        previous, current = (current, following)
    return (previous, current)


def solution(mesh):
    return jax.shard_map(
        on_device,
        mesh=mesh,
        in_specs=(
            P("gx", "gy", None),
            P("gx", "gy", None),
            P("gx", "gy", None),
            P(("gx", "gy"), None),
            P(("gx", "gy"), None),
            P(("gx", "gy")),
            P(("gx", "gy"), None),
        ),
        out_specs=(P("gx", "gy", None), P("gx", "gy", None)),
        check_vma=False,
    )
```

profile of v0, /device:TPU:10, one launch (start us, length us, event | category | flops | bytes accessed | tf_op | source)
XLA Modules:
  0.0 552.4 jit_solution(2218229386027490389)
XLA Ops:
  0.7 2.6 convert_reduce_fusion
  3.2 6.5 %sort.17 = (s32[4096]{0:T(1024)}, s32[4096]{0:T(1024)S(1)}) sort(s32[4096]{0:T(1024)} %bitcast.22, s32[4096]{0:T(1024)S(1)} %iota.16), dimensions={0}, to_apply=%region_0.0 | sort | flops 49152 | bytes 65536 | tf_op jit(solution)/shard_map/jit(argsort)/sort | solution.py:67
  9.7 23.0 %gather_fusion = s32[4096]{0:T(1024)S(1)} fusion(s32[4096]{0:T(1024)S(1)} %bitcast.23, s32[4096]{0:T(1024)S(1)} %fusion.136), kind=kCustom, calls=%fused_computation | custom fusion | bytes 49152 | tf_op jit(solution)/shard_map/gather | solution.py:68
  33.2 1.3 select_reduce_fusion
  34.5 23.0 %gather_fusion.1 = s32[4096]{0:T(1024)S(1)} fusion(s32[4096]{0:T(1024)S(1)} %copy-done.3, s32[4096]{0:T(1024)S(1)} %fusion.136), kind=kCustom, calls=%fused_computation.1 | custom fusion | bytes 49152 | tf_op jit(solution)/shard_map/gather | solution.py:79
  57.6 15.5 %scatter_custom_fusion = s32[8192]{0:T(1024)S(1)} fusion(s32[4096]{0:T(1024)S(1)} %bitcast.35, s32[4096]{0:T(1024)S(1)} %gather_fusion.1, s32[]{:T(128)} %constant.7.clone.1), kind=kCustom, calls=%fused_computation.255 | custom fusion | bytes 32772 | tf_op jit(solution)/shard_map/scatter | solution.py:79
  73.8 10.4 %all-to-all-start = ((s32[128,1,64]{2,1,0:T(1,128)}), s32[128,1,64]{2,1,0:T(1,128)S(1)}, u32[]{:S(2)}, u32[]{:S(2)}) async-start(s32[128,1,64]{2,1,0:T(1,128)} %bitcast.5), calls=%async_computation | async-start | bytes 131072 | tf_op jit(solution)/shard_map/all_to_all | solution.py:88
  84.3 2.1 fusion.143
  86.4 2.2 collective-permute-start
  88.6 2.6 collective-permute-start.1
  91.2 8.0 %constant_dynamic-update-slice_fusion.1 = (f32[36,64,512]{2,0,1:T(8,128)}, f32[32,64,512]{2,0,1:T(8,128)}) fusion(f32[32,64,512]{2,1,0:T(8,128)} %param.8), kind=kLoop, calls=%fused_computation.259 | loop fusion | bytes 12582912
  99.2 24.6 %scatter_custom_fusion.1 = bf16[8192,128]{1,0:T(8,128)(2,1)} fusion(s32[4096]{0:T(1024)S(1)} %bitcast.36, bf16[4096,128]{1,0:T(8,128)(2,1)S(1)} %copy-done, s32[4096]{0:T(1024)S(1)} %fusion.136, bf16[]{:T(256)} %constant.12.clone.1), kind=kCustom, calls=%fused_computation.235 | custom fusion | bytes 2097154 | tf_op jit(solution)/shard_map/scatter | solution.py:77
  124.2 10.8 %all-to-all-start.1 = ((bf16[128,64,128]{2,1,0:T(8,128)(2,1)}), bf16[128,64,128]{2,1,0:T(8,128)(2,1)S(1)}, u32[]{:S(2)}, u32[]{:S(2)}) async-start(bf16[128,64,128]{2,1,0:T(8,128)(2,1)} %bitcast.7), calls=%async_computation.1 | async-start | bytes 4194304 | tf_op jit(solution)/shard_map/all_to_all | solution.py:81
  135.0 2.3 constant_dynamic-update-slice_fusion
  137.2 2.0 pad_maximum_fusion.20
  139.2 5.2 collective-permute-start.2
  144.5 2.1 collective-permute-start.3
  147.3 0.8 multiply_reduce_fusion
  148.1 0.9 mul.128
  149.8 17.0 %collective-permute-done.2 = f32[40,4,512]{2,0,1:T(8,128)S(1)} collective-permute-done((f32[40,4,512]{2,0,1:T(8,128)}, f32[40,4,512]{2,0,1:T(8,128)S(1)}, u32[]{:S(2)}, u32[]{:S(2)}) %collective-permute-start.2) | collective-permute-done | bytes 327712 | tf_op jit(solution)/shard_map/ppermute | solution.py:21
  166.8 2.5 collective-permute-done.3
  169.3 7.4 %pad_maximum_fusion = (f32[40,68,512]{2,0,1:T(8,128)}, f32[40,68,512]{2,0,1:T(8,128)}) fusion(f32[40,4,512]{2,0,1:T(8,128)S(1)} %collective-permute-done.2, f32[4,64,512]{2,0,1:T(4,128)S(1)} %get-tuple-element.41, f32[32,64,512]{2,0,1:T(8,128)} %get-tuple-element.37, f32[4,64,512]{2,0,1:T(4,128)S(1)} %copy.78, f32[40,4,512]{2,0,1:T(8,128)} %collective-permute-done.3), kind=kLoop, calls=%fused_computation.67 | loop fusion | flops 8355840 | bytes 17039360 | tf_op jit(solution)/shard_map/concatenate | solution.py:22
  176.8 9.8 %select_maximum_fusion.12 = f32[40,72,520]{2,0,1:T(8,128)} fusion(f32[40,4,512]{2,0,1:T(8,128)S(1)} %collective-permute-done.2, f32[40,4,512]{2,0,1:T(8,128)} %collective-permute-done.3, f32[4,64,512]{2,0,1:T(4,128)S(1)} %get-tuple-element.41, f32[32,64,512]{2,0,1:T(8,128)S(1)} %copy-done.7, f32[4,64,512]{2,0,1:T(4,128)S(1)} %copy.78), kind=kLoop, calls=%fused_computation.41 | loop fusion | flops 17971200 | bytes 11888640 | tf_op jit(solution)/shard_map/concatenate | solution.py:22
  186.5 55.2 %scatter_custom_fusion.2 = f32[16384,128]{1,0:T(8,128)} fusion(s32[8192]{0:T(1024)S(1)} %bitcast.34, bf16[8192,128]{1,0:T(8,128)(2,1)S(1)} %bitcast.30, f32[]{:T(128)} %constant.15.clone.1), kind=kCustom, calls=%fused_computation.227 | custom fusion | flops 2097152 | bytes 10485764 | tf_op jit(solution)/shard_map/scatter-add | solution.py:100
  241.7 5.1 convert_element_type.23
  246.8 7.4 %convert_element_type.24 = bf16[2048,1024]{1,0:T(8,128)(2,1)} reshape(bf16[16384,128]{1,0:T(8,128)(2,1)} %convert_element_type.23) | data formatting | bytes 8388608 | tf_op jit(solution)/shard_map/convert_element_type | solution.py:105
  254.3 15.4 %fusion.144 = f32[2048,2048]{1,0:T(8,128)} fusion(bf16[2048,1024]{1,0:T(8,128)(2,1)} %convert_element_type.24, bf16[1024,2048]{1,0:T(8,128)(2,1)} %param.13), kind=kOutput, calls=%fused_computation.265 | convolution fusion | flops 8589934592 | bytes 25165824 | tf_op jit(solution)/shard_map/dot_general | solution.py:106
  269.6 12.5 %fusion.139 = (f32[2048,512]{1,0:T(8,128)}, f32[2048,512]{1,0:T(8,128)}, f32[2048,512]{1,0:T(8,128)}, f32[2048,512]{1,0:T(8,128)}) fusion(f32[2048,2048]{1,0:T(8,128)} %fusion.144), kind=kLoop, calls=%fused_computation.260 | loop fusion | bytes 33554432 | tf_op jit(solution)/shard_map/slice | solution.py:109
  282.2 41.9 %fusion.105 = f32[32,64,512]{2,0,1:T(8,128)S(1)} fusion(f32[32,64,512]{2,0,1:T(8,128)S(1)} %copy-done.8, f32[4,64,512]{2,0,1:T(4,128)S(1)} %copy-done.10, f32[40,72,520]{2,0,1:T(8,128)S(1)} %bitcast.25, f32[40,68,512]{2,0,1:T(8,128)} %get-tuple-element.27, f32[40,68,512]{2,0,1:T(8,128)} %get-tuple-element.26, f32[36,64,512]{2,0,1:T(8,128)} %get-tuple-element.40, ...), kind=kLoop, calls=%fused_computation.179 | loop fusion | flops 39845888 | bytes 105381888 | tf_op jit(solution)/shard_map/add | solution.py:114
  324.5 1.9 collective-permute-start.4
  326.6 2.4 collective-permute-start.5
  329.0 4.1 collective-permute-done.4
  333.4 3.7 collective-permute-done.5
  337.5 2.7 collective-permute-start.6
  340.2 3.4 collective-permute-start.7
  343.7 3.4 collective-permute-done.6
  347.1 4.5 collective-permute-done.7
  351.6 5.5 pad_maximum_fusion.1
  357.1 8.4 %select_maximum_fusion.8 = f32[40,72,520]{2,0,1:T(8,128)S(1)} fusion(f32[40,4,512]{2,0,1:T(8,128)S(1)} %collective-permute-done.6, f32[40,4,512]{2,0,1:T(8,128)S(1)} %collective-permute-done.7, f32[4,64,512]{2,0,1:T(4,128)S(1)} %copy.89, f32[32,64,512]{2,0,1:T(8,128)} %copy-done.4, f32[4,64,512]{2,0,1:T(4,128)S(1)} %copy.91), kind=kLoop, calls=%fused_computation.37 | loop fusion | flops 17971200 | bytes 11888640 | tf_op jit(solution)/shard_map/concatenate | solution.py:22
  365.5 27.6 %fusion.74 = f32[32,64,512]{2,0,1:T(8,128)S(1)} fusion(f32[32,64,512]{2,0,1:T(8,128)S(1)} %copy-done.5, f32[4,64,512]{2,0,1:T(4,128)S(1)} %copy.91, f32[4,64,512]{2,0,1:T(4,128)S(1)} %copy.89, f32[40,72,520]{2,0,1:T(8,128)S(1)} %select_maximum_fusion.8, f32[40,68,512]{2,0,1:T(8,128)} %get-tuple-element.23, f32[40,68,512]{2,0,1:T(8,128)} %get-tuple-element.22, ...), kind=kLoop, calls=%fused_computation.148 | loop fusion | flops 44040192 | bytes 89128960 | tf_op jit(solution)/shard_map/add | solution.py:114
  393.6 1.9 collective-permute-start.8
  395.7 2.4 collective-permute-start.9
  398.1 4.1 collective-permute-done.8
  402.5 3.7 collective-permute-done.9
  406.6 1.9 collective-permute-start.10
  408.6 4.4 collective-permute-start.11
  413.0 5.2 collective-permute-done.10
  418.2 4.0 collective-permute-done.11
  422.2 5.5 pad_maximum_fusion.2
  427.7 7.3 %select_maximum_fusion.4 = f32[40,72,520]{2,0,1:T(8,128)S(1)} fusion(f32[40,4,512]{2,0,1:T(8,128)S(1)} %collective-permute-done.10, f32[40,4,512]{2,0,1:T(8,128)S(1)} %collective-permute-done.11, f32[4,64,512]{2,0,1:T(4,128)S(1)} %copy.97, f32[32,64,512]{2,0,1:T(8,128)S(1)} %fusion.74, f32[4,64,512]{2,0,1:T(4,128)S(1)} %copy.99), kind=kLoop, calls=%fused_computation.33 | loop fusion | flops 17971200 | bytes 11888640 | tf_op jit(solution)/shard_map/concatenate | solution.py:22
  435.1 27.0 %fusion.43 = f32[32,64,512]{2,0,1:T(8,128)} fusion(f32[32,64,512]{2,0,1:T(8,128)S(1)} %fusion.74, f32[4,64,512]{2,0,1:T(4,128)S(1)} %copy.99, f32[4,64,512]{2,0,1:T(4,128)S(1)} %copy.97, f32[40,72,520]{2,0,1:T(8,128)S(1)} %select_maximum_fusion.4, f32[40,68,512]{2,0,1:T(8,128)} %get-tuple-element.19, f32[40,68,512]{2,0,1:T(8,128)} %get-tuple-element.18, ...), kind=kLoop, calls=%fused_computation.117 | loop fusion | flops 44040192 | bytes 89128960 | tf_op jit(solution)/shard_map/add | solution.py:114
  462.1 1.9 fusion.140
  464.2 1.9 collective-permute-start.12
  466.3 2.4 collective-permute-start.13
  468.7 4.1 collective-permute-done.12
  473.1 3.7 collective-permute-done.13
  477.3 1.9 collective-permute-start.14
  479.2 4.1 collective-permute-start.15
  483.3 4.4 copy.112
  487.7 3.5 collective-permute-done.15
  491.2 5.6 %pad_maximum_fusion.3 = (f32[40,68,512]{2,0,1:T(8,128)}, f32[40,68,512]{2,0,1:T(8,128)}) fusion(f32[40,4,512]{2,0,1:T(8,128)S(1)} %collective-permute-done.14, f32[4,64,512]{2,0,1:T(4,128)S(1)} %copy.105, f32[32,64,512]{2,0,1:T(8,128)S(1)} %copy-done.6, f32[4,64,512]{2,0,1:T(4,128)S(1)} %copy.107, f32[40,4,512]{2,0,1:T(8,128)S(1)} %collective-permute-done.15), kind=kLoop, calls=%fused_computation.73 | loop fusion | flops 8355840 | bytes 17039360 | tf_op jit(solution)/shard_map/concatenate | solution.py:22
  496.8 7.3 %select_maximum_fusion = f32[40,72,520]{2,0,1:T(8,128)S(1)} fusion(f32[40,4,512]{2,0,1:T(8,128)S(1)} %collective-permute-done.14, f32[40,4,512]{2,0,1:T(8,128)S(1)} %collective-permute-done.15, f32[4,64,512]{2,0,1:T(4,128)S(1)} %copy.105, f32[32,64,512]{2,0,1:T(8,128)S(1)} %copy-done.6, f32[4,64,512]{2,0,1:T(4,128)S(1)} %copy.107), kind=kLoop, calls=%fused_computation.29 | loop fusion | flops 17971200 | bytes 11888640 | tf_op jit(solution)/shard_map/concatenate | solution.py:22
  504.2 41.4 %fusion.12 = f32[32,64,512]{2,0,1:T(8,128)} fusion(f32[32,64,512]{2,0,1:T(8,128)} %fusion.43, f32[4,64,512]{2,0,1:T(4,128)S(1)} %copy.107, f32[4,64,512]{2,0,1:T(4,128)S(1)} %copy.105, f32[40,72,520]{2,0,1:T(8,128)S(1)} %select_maximum_fusion, f32[40,68,512]{2,0,1:T(8,128)} %get-tuple-element.15, f32[40,68,512]{2,0,1:T(8,128)} %get-tuple-element.14, ...), kind=kLoop, calls=%fused_computation.86 | loop fusion | flops 44040192 | bytes 89128960 | tf_op jit(solution)/shard_map/add | solution.py:114
  545.6 6.6 %copy.113 = f32[32,64,512]{2,1,0:T(8,128)} copy(f32[32,64,512]{2,0,1:T(8,128)} %fusion.12) | data formatting | bytes 8388608
  (62 shorter events, 6.9 us)
Async XLA Ops:
  0.6 98.6 %copy-start = (bf16[4096,128]{1,0:T(8,128)(2,1)S(1)}, bf16[4096,128]{1,0:T(8,128)(2,1)}, u32[]{:S(2)}) copy-start(bf16[4096,128]{1,0:T(8,128)(2,1)} %param.10) | copy-start | bytes 3145732
  0.6 9.1 %copy-start.2 = (s32[4096,1]{0,1:T(1,128)S(1)}, s32[4096,1]{0,1:T(1,128)}, u32[]{:S(2)}) copy-start(s32[4096,1]{0,1:T(1,128)} %param.11) | copy-start | bytes 49156
  32.8 1.7 copy-start.3
  73.8 50.4 %all-to-all-start = ((s32[128,1,64]{2,1,0:T(1,128)}), s32[128,1,64]{2,1,0:T(1,128)S(1)}, u32[]{:S(2)}, u32[]{:S(2)}) async-start(s32[128,1,64]{2,1,0:T(1,128)} %bitcast.5), calls=%async_computation | async-start | bytes 131072 | tf_op jit(solution)/shard_map/all_to_all | solution.py:88
  86.4 48.6 %collective-permute-start = (f32[4,64,512]{2,1,0:T(8,128)}, f32[4,64,512]{2,1,0:T(8,128)}, u32[]{:S(2)}, u32[]{:S(2)}) collective-permute-start(f32[4,64,512]{2,1,0:T(8,128)} %get-tuple-element.38), channel_id=1, source_target_pairs={{16,0},{32,16},{48,32},{64,48},{80,64},{96,80},{112,96},{17,1},{33... | collective-permute-start | bytes 1572872 | tf_op jit(solution)/shard_map/ppermute | solution.py:21
  88.6 35.3 %collective-permute-start.1 = (f32[4,64,512]{2,1,0:T(8,128)S(1)}, f32[4,64,512]{2,1,0:T(8,128)S(1)}, u32[]{:S(2)}, u32[]{:S(2)}) collective-permute-start(f32[4,64,512]{2,1,0:T(8,128)S(1)} %get-tuple-element.39), channel_id=1, source_target_pairs={{0,16},{16,32},{32,48},{48,64},{64,80},{80,96},{96,112},{1,17},{17... | collective-permute-start | bytes 1572872 | tf_op jit(solution)/shard_map/ppermute | solution.py:18
  124.2 52.6 %copy-start.9 = (f32[4,64,512]{2,0,1:T(4,128)}, f32[4,64,512]{2,0,1:T(4,128)S(1)}, u32[]{:S(2)}) copy-start(f32[4,64,512]{2,0,1:T(4,128)S(1)} %copy.78) | copy-start | bytes 1572868
  124.2 62.3 %all-to-all-start.1 = ((bf16[128,64,128]{2,1,0:T(8,128)(2,1)}), bf16[128,64,128]{2,1,0:T(8,128)(2,1)S(1)}, u32[]{:S(2)}, u32[]{:S(2)}) async-start(bf16[128,64,128]{2,1,0:T(8,128)(2,1)} %bitcast.7), calls=%async_computation.1 | async-start | bytes 4194304 | tf_op jit(solution)/shard_map/all_to_all | solution.py:81
  139.2 27.5 %collective-permute-start.2 = (f32[40,4,512]{2,0,1:T(8,128)}, f32[40,4,512]{2,0,1:T(8,128)S(1)}, u32[]{:S(2)}, u32[]{:S(2)}) collective-permute-start(f32[40,4,512]{2,0,1:T(8,128)} %get-tuple-element.29), channel_id=1, source_target_pairs={{1,0},{2,1},{3,2},{4,3},{5,4},{6,5},{7,6},{8,7},{9,8},{10,9},{11,1... | collective-permute-start | bytes 983048 | tf_op jit(solution)/shard_map/ppermute | solution.py:21
  144.5 24.8 %collective-permute-start.3 = (f32[40,4,512]{2,0,1:T(8,128)}, f32[40,4,512]{2,0,1:T(8,128)}, u32[]{:S(2)}, u32[]{:S(2)}) collective-permute-start(f32[40,4,512]{2,0,1:T(8,128)} %get-tuple-element.28), channel_id=1, source_target_pairs={{0,1},{1,2},{2,3},{3,4},{4,5},{5,6},{6,7},{7,8},{8,9},{9,10},{10,1... | collective-permute-start | bytes 983048 | tf_op jit(solution)/shard_map/ppermute | solution.py:18
  149.8 26.9 %copy-start.7 = (f32[32,64,512]{2,0,1:T(8,128)S(1)}, f32[32,64,512]{2,0,1:T(8,128)}, u32[]{:S(2)}) copy-start(f32[32,64,512]{2,0,1:T(8,128)} %get-tuple-element.37) | copy-start | bytes 12582916
  246.8 35.3 %slice-start = ((s8[7372800]{0:T(1024)(128)(4,1)}), s8[3178496]{0:T(1024)(128)(4,1)S(1)}, s32[]{:S(2)}) async-start(s8[7372800]{0:T(1024)(128)(4,1)} %bitcast.24), calls=%async_computation.2 | async-start | bytes 6356992
  254.3 27.9 %slice-start.1 = ((s8[7372800]{0:T(1024)(128)(4,1)}), s8[4194304]{0:T(1024)(128)(4,1)S(1)}, s32[]{:S(2)}) async-start(s8[7372800]{0:T(1024)(128)(4,1)} %bitcast.24), calls=%async_computation.3 | async-start | bytes 8388608
  269.6 12.5 %copy-start.8 = (f32[32,64,512]{2,0,1:T(8,128)S(1)}, f32[32,64,512]{2,0,1:T(8,128)}, u32[]{:S(2)}) copy-start(f32[32,64,512]{2,0,1:T(8,128)} %get-tuple-element.37) | copy-start | bytes 12582916
  269.6 12.5 %copy-start.10 = (f32[4,64,512]{2,0,1:T(4,128)S(1)}, f32[4,64,512]{2,0,1:T(4,128)}, u32[]{:S(2)}) copy-start(f32[4,64,512]{2,0,1:T(4,128)} %copy-done.9) | copy-start | bytes 1572868
  324.0 27.6 %copy-start.4 = (f32[32,64,512]{2,0,1:T(8,128)}, f32[32,64,512]{2,0,1:T(8,128)S(1)}, u32[]{:S(2)}) copy-start(f32[32,64,512]{2,0,1:T(8,128)S(1)} %fusion.105) | copy-start | bytes 12582916
  324.5 8.6 %collective-permute-start.4 = (f32[4,64,512]{2,1,0:T(8,128)S(1)}, f32[4,64,512]{2,1,0:T(8,128)S(1)}, u32[]{:S(2)}, u32[]{:S(2)}) collective-permute-start(f32[4,64,512]{2,1,0:T(8,128)S(1)} %copy.88), channel_id=1, source_target_pairs={{16,0},{32,16},{48,32},{64,48},{80,64},{96,80},{112,96},{17,1},{33... | collective-permute-start | bytes 1572872 | tf_op jit(solution)/shard_map/ppermute | solution.py:21
  326.6 10.5 %collective-permute-start.5 = (f32[4,64,512]{2,1,0:T(8,128)S(1)}, f32[4,64,512]{2,1,0:T(8,128)S(1)}, u32[]{:S(2)}, u32[]{:S(2)}) collective-permute-start(f32[4,64,512]{2,1,0:T(8,128)S(1)} %copy.90), channel_id=1, source_target_pairs={{0,16},{16,32},{32,48},{48,64},{64,80},{80,96},{96,112},{1,17},{17... | collective-permute-start | bytes 1572872 | tf_op jit(solution)/shard_map/ppermute | solution.py:18
  337.5 9.5 %collective-permute-start.6 = (f32[40,4,512]{2,0,1:T(8,128)S(1)}, f32[40,4,512]{2,0,1:T(8,128)S(1)}, u32[]{:S(2)}, u32[]{:S(2)}) collective-permute-start(f32[40,4,512]{2,0,1:T(8,128)S(1)} %get-tuple-element.25), channel_id=1, source_target_pairs={{1,0},{2,1},{3,2},{4,3},{5,4},{6,5},{7,6},{8,7},{9,8},{10,9},{11,1... | collective-permute-start | bytes 983048 | tf_op jit(solution)/shard_map/ppermute | solution.py:21
  340.2 11.4 %collective-permute-start.7 = (f32[40,4,512]{2,0,1:T(8,128)S(1)}, f32[40,4,512]{2,0,1:T(8,128)S(1)}, u32[]{:S(2)}, u32[]{:S(2)}) collective-permute-start(f32[40,4,512]{2,0,1:T(8,128)S(1)} %get-tuple-element.24), channel_id=1, source_target_pairs={{0,1},{1,2},{2,3},{3,4},{4,5},{5,6},{6,7},{7,8},{8,9},{9,10},{10,1... | collective-permute-start | bytes 983048 | tf_op jit(solution)/shard_map/ppermute | solution.py:18
  357.1 8.4 %copy-start.5 = (f32[32,64,512]{2,0,1:T(8,128)S(1)}, f32[32,64,512]{2,0,1:T(8,128)}, u32[]{:S(2)}) copy-start(f32[32,64,512]{2,0,1:T(8,128)} %copy-done.4) | copy-start | bytes 12582916
  393.6 8.6 %collective-permute-start.8 = (f32[4,64,512]{2,1,0:T(8,128)S(1)}, f32[4,64,512]{2,1,0:T(8,128)S(1)}, u32[]{:S(2)}, u32[]{:S(2)}) collective-permute-start(f32[4,64,512]{2,1,0:T(8,128)S(1)} %copy.96), channel_id=1, source_target_pairs={{16,0},{32,16},{48,32},{64,48},{80,64},{96,80},{112,96},{17,1},{33... | collective-permute-start | bytes 1572872 | tf_op jit(solution)/shard_map/ppermute | solution.py:21
  395.7 10.5 %collective-permute-start.9 = (f32[4,64,512]{2,1,0:T(8,128)S(1)}, f32[4,64,512]{2,1,0:T(8,128)S(1)}, u32[]{:S(2)}, u32[]{:S(2)}) collective-permute-start(f32[4,64,512]{2,1,0:T(8,128)S(1)} %copy.98), channel_id=1, source_target_pairs={{0,16},{16,32},{32,48},{48,64},{64,80},{80,96},{96,112},{1,17},{17... | collective-permute-start | bytes 1572872 | tf_op jit(solution)/shard_map/ppermute | solution.py:18
  406.6 11.5 %collective-permute-start.10 = (f32[40,4,512]{2,0,1:T(8,128)S(1)}, f32[40,4,512]{2,0,1:T(8,128)S(1)}, u32[]{:S(2)}, u32[]{:S(2)}) collective-permute-start(f32[40,4,512]{2,0,1:T(8,128)S(1)} %get-tuple-element.21), channel_id=1, source_target_pairs={{1,0},{2,1},{3,2},{4,3},{5,4},{6,5},{7,6},{8,7},{9,8},{10,9},{11,1... | collective-permute-start | bytes 983048 | tf_op jit(solution)/shard_map/ppermute | solution.py:21
  408.6 13.7 %collective-permute-start.11 = (f32[40,4,512]{2,0,1:T(8,128)S(1)}, f32[40,4,512]{2,0,1:T(8,128)S(1)}, u32[]{:S(2)}, u32[]{:S(2)}) collective-permute-start(f32[40,4,512]{2,0,1:T(8,128)S(1)} %get-tuple-element.20), channel_id=1, source_target_pairs={{0,1},{1,2},{2,3},{3,4},{4,5},{5,6},{6,7},{7,8},{8,9},{9,10},{10,1... | collective-permute-start | bytes 983048 | tf_op jit(solution)/shard_map/ppermute | solution.py:18
  462.1 15.1 %copy-start.6 = (f32[32,64,512]{2,0,1:T(8,128)S(1)}, f32[32,64,512]{2,0,1:T(8,128)}, u32[]{:S(2)}) copy-start(f32[32,64,512]{2,0,1:T(8,128)} %fusion.43) | copy-start | bytes 12582916
  464.2 8.6 %collective-permute-start.12 = (f32[4,64,512]{2,1,0:T(8,128)S(1)}, f32[4,64,512]{2,1,0:T(8,128)S(1)}, u32[]{:S(2)}, u32[]{:S(2)}) collective-permute-start(f32[4,64,512]{2,1,0:T(8,128)S(1)} %copy.104), channel_id=1, source_target_pairs={{16,0},{32,16},{48,32},{64,48},{80,64},{96,80},{112,96},{17,1},{33... | collective-permute-start | bytes 1572872 | tf_op jit(solution)/shard_map/ppermute | solution.py:21
  466.3 10.5 %collective-permute-start.13 = (f32[4,64,512]{2,1,0:T(8,128)S(1)}, f32[4,64,512]{2,1,0:T(8,128)S(1)}, u32[]{:S(2)}, u32[]{:S(2)}) collective-permute-start(f32[4,64,512]{2,1,0:T(8,128)S(1)} %copy.106), channel_id=1, source_target_pairs={{0,16},{16,32},{32,48},{48,64},{64,80},{80,96},{96,112},{1,17},{17... | collective-permute-start | bytes 1572872 | tf_op jit(solution)/shard_map/ppermute | solution.py:18
  477.3 10.5 %collective-permute-start.14 = (f32[40,4,512]{2,0,1:T(8,128)S(1)}, f32[40,4,512]{2,0,1:T(8,128)S(1)}, u32[]{:S(2)}, u32[]{:S(2)}) collective-permute-start(f32[40,4,512]{2,0,1:T(8,128)S(1)} %get-tuple-element.17), channel_id=1, source_target_pairs={{1,0},{2,1},{3,2},{4,3},{5,4},{6,5},{7,6},{8,7},{9,8},{10,9},{11,1... | collective-permute-start | bytes 983048 | tf_op jit(solution)/shard_map/ppermute | solution.py:21
  479.2 12.1 %collective-permute-start.15 = (f32[40,4,512]{2,0,1:T(8,128)S(1)}, f32[40,4,512]{2,0,1:T(8,128)S(1)}, u32[]{:S(2)}, u32[]{:S(2)}) collective-permute-start(f32[40,4,512]{2,0,1:T(8,128)S(1)} %get-tuple-element.16), channel_id=1, source_target_pairs={{0,1},{1,2},{2,3},{3,4},{4,5},{5,6},{6,7},{7,8},{8,9},{9,10},{10,1... | collective-permute-start | bytes 983048 | tf_op jit(solution)/shard_map/ppermute | solution.py:18
  504.2 48.0 %copy-start.1 = (bf16[4096,128]{1,0:T(8,128)(2,1)S(1)}, bf16[4096,128]{1,0:T(8,128)(2,1)}, u32[]{:S(2)}) copy-start(bf16[4096,128]{1,0:T(8,128)(2,1)} %param.10) | copy-start | bytes 3145732
where the time goes:
time: 558 us; the launch traced here: 552 us
  other arithmetic  270 us (48%)
  local copies, waits for them, and re-layouts  138 us (25%)
  starting transfers between devices  64.7 us (12%)
  waiting for transfers between devices  63.4 us (11%)
  matrix products  15.4 us (3%)
    add x4, other arithmetic, on_device(): 2.0 * current - previous  138 us
    concatenate x12, other arithmetic, padded_2(): block = jnp.concatenate([low, block, high], axis=dim)  59.1 us
    scatter-add x1, other arithmetic, on_device(): jax.ops.segment_sum(got_rows.reshape(-1, samples).astype(jnp.float32), se...  55.2 us
    ppermute x8, waiting for transfers between devices, padded_2(): lax.ppermute(lax.slice_in_dim(block, 0, width, axis=dim), axis, backward)  37.9 us
    ppermute x8, waiting for transfers between devices, padded_2(): lax.ppermute(lax.slice_in_dim(block, block.shape[dim] - width, None, axis...  25.6 us
    scatter x1, local copies, waits for them, and re-layouts, on_device(): jnp.zeros((devices * capacity, samples), traces.dtype).at[slot_index]  24.6 us
    ppermute x8, starting transfers between devices, padded_2(): lax.ppermute(lax.slice_in_dim(block, block.shape[dim] - width, None, axis...  23.9 us
    gather x1, local copies, waits for them, and re-layouts, on_device(): sorted_target = target[ordering]  23 us
  transfers between devices with their start and end apart: 18, of which 13 were waited for; matrix products, arithmetic and copies ran while one was open for 12% of the time, Pallas kernels for 0%

commit v1 on v0

v1 whole, which is shorter than its diff:
```python
import jax
import jax.numpy as jnp
from jax import lax
from jax.experimental import pallas as pl
from jax.experimental.pallas import tpu as pltpu
from jax.sharding import PartitionSpec as P

STEPS = 4
MESH = pl.DeviceIdType.MESH
F32 = jnp.float32
BF16 = jnp.bfloat16
LANES = 128
SLOTS = 64
MSG = 72
EDGE = 4
PLANES = 4

CENTER5 = 3.0 * -205.0 / 72.0 * 5.0
SIDE5 = (8.0, -1.0, 8.0 / 63.0, -1.0 / 112.0)


def iota(shape, dim):
    return lax.broadcasted_iota(jnp.int32, shape, dim)


def pack_kernel(owner_ref, cell_ref, trace_ref, out_ref, wide, rows32, slots_v, slots_s, cells_v, sem):
    blocks = owner_ref.shape[0]
    owners = out_ref.shape[0]
    before = (iota((LANES, 2 * LANES), 0) < iota((LANES, 2 * LANES), 1)).astype(F32).astype(BF16)
    carry = jnp.zeros((owners, LANES), F32)
    cells = jnp.zeros((owners, 2 * SLOTS), F32)
    for i in range(blocks):
        own = owner_ref[i : i + 1, :]
        cell = cell_ref[i : i + 1, :]
        hot = (own == iota((owners, LANES), 0)).astype(F32)
        hot16 = hot.astype(BF16)
        seen = jnp.dot(hot16, before, preferred_element_type=F32)
        rank = jnp.sum(hot * (seen[:, :LANES] + carry), axis=0, keepdims=True)
        carry = carry + seen[:, LANES:]
        rank = rank.astype(jnp.int32)
        slots_v[i : i + 1, :] = own * SLOTS + rank
        high = ((cell // SLOTS) + 1).astype(F32)
        low = (cell % SLOTS).astype(F32)
        place = iota((2 * SLOTS, LANES), 0)
        digit = jnp.where(place < SLOTS, high, low)
        digit = jnp.where(place % SLOTS == rank, digit, 0.0).astype(BF16)
        cells = cells + lax.dot_general(
            hot16, digit, (((1,), (1,)), ((), ())), preferred_element_type=F32
        )
    cells_v[...] = cells
    copy = pltpu.make_async_copy(slots_v, slots_s, sem)
    copy.start()

    @pl.loop(0, owners)
    def _(o):
        at = pl.multiple_of(o * SLOTS, SLOTS)
        wide[pl.ds(at, SLOTS), :] = jnp.zeros((SLOTS, LANES), F32)

    rows32[...] = trace_ref[...].astype(F32)
    copy.wait()

    @pl.loop(0, blocks)
    def _(i):
        base = pl.multiple_of(i * LANES, LANES)
        for j in range(LANES):
            wide[pl.ds(slots_s[i, j], 1), :] = rows32[pl.ds(base + j, 1), :]

    @pl.loop(0, owners)
    def _(o):
        at = pl.multiple_of(o * SLOTS, SLOTS)
        out_ref[o, :SLOTS, :] = wide[pl.ds(at, SLOTS), :].astype(BF16)
        out_ref[o, SLOTS:, :] = jnp.broadcast_to(cells_v[pl.ds(o, 1), :], (MSG - SLOTS, LANES)).astype(BF16)


def pack(owner, cell, traces, owners):
    rows = traces.shape[0]
    blocks = rows // LANES
    vmem = pl.BlockSpec(memory_space=pltpu.VMEM)
    return pl.pallas_call(
        pack_kernel,
        out_shape=jax.ShapeDtypeStruct((owners, MSG, LANES), BF16),
        in_specs=[vmem] * 3,
        out_specs=vmem,
        scratch_shapes=[
            pltpu.VMEM((owners * SLOTS, LANES), F32),
            pltpu.VMEM((rows, LANES), F32),
            pltpu.VMEM((blocks, LANES), jnp.int32),
            pltpu.SMEM((blocks, LANES), jnp.int32),
            pltpu.VMEM((owners, 2 * SLOTS), F32),
            pltpu.SemaphoreType.DMA,
        ],
        compiler_params=pltpu.CompilerParams(vmem_limit_bytes=32 << 20),
    )(owner, cell, traces)


def sum_slab(rows, gath, g, sources):
    cell_count = gath.shape[1]
    lane = iota((1, LANES), 1)
    highs, spots, values = [], [], []
    for i in range(0, sources, 2):
        one = rows[g * sources + i, SLOTS:, :].astype(F32)[:1, :]
        two = rows[g * sources + i + 1, SLOTS:, :].astype(F32)[:1, :]
        high = jnp.where(lane < SLOTS, one, pltpu.roll(two, SLOTS, 1))
        low = jnp.where(lane < SLOTS, pltpu.roll(one, SLOTS, 1), two)
        highs.append(high)
        spots.append((iota((SLOTS, LANES), 0).astype(F32) == low).astype(F32).astype(BF16))
        values.append(rows[g * sources + i, :SLOTS, :])
        values.append(rows[g * sources + i + 1, :SLOTS, :])
    high = jnp.concatenate(highs, axis=1)
    spot = jnp.concatenate(spots, axis=1)
    value = jnp.concatenate(values, axis=0)
    part = 8
    for first in range(0, cell_count // SLOTS, part):
        picked = []
        for h in range(first, first + part):
            here = (high == float(h + 1)).astype(F32).astype(BF16)
            picked.append(spot * jnp.broadcast_to(here, spot.shape))
        hot = jnp.concatenate(picked, axis=0)
        total = jnp.dot(hot, value, preferred_element_type=F32)
        gath[g, first * SLOTS : (first + part) * SLOTS, :] = total.astype(BF16)


def wave_kernel(
    prev_ref, now_ref, courant_ref, rows, green_ref, before_ref, after_ref,
    first, second, speed, gath, green, inject, along, band, ysend, yrecv,
    load_sem, store_sem, send_sem, recv_sem,
):
    gx, gy = lax.axis_index("gx"), lax.axis_index("gy")
    nx, ny = lax.axis_size("gx"), lax.axis_size("gy")
    size_x, size_y, size_z = now_ref.shape
    tiles = size_z // LANES
    halves = (first, second)
    low_y = 2 * EDGE
    inner = pl.ds(low_y, size_y)
    near = (
        (gx > 0, (lax.rem(gx + nx - 1, nx), gy)),
        (gx < nx - 1, (lax.rem(gx + 1, nx), gy)),
        (gy > 0, (gx, lax.rem(gy + ny - 1, ny))),
        (gy < ny - 1, (gx, lax.rem(gy + 1, ny))),
    )

    loads = []
    for i, (source, target) in enumerate(((now_ref, first), (prev_ref, second))):
        for k in range(tiles):
            loads.append(
                pltpu.make_async_copy(
                    source.at[:, :, pl.ds(k * LANES, LANES)],
                    target.at[pl.ds(EDGE, size_x), k, inner, :],
                    load_sem.at[i * tiles + k],
                )
            )
    for k in range(tiles):
        loads.append(
            pltpu.make_async_copy(
                courant_ref.at[:, :, pl.ds(k * LANES, LANES)], speed.at[:, k], load_sem.at[2 * tiles + k]
            )
        )
    loads.append(pltpu.make_async_copy(green_ref, green, load_sem.at[3 * tiles]))
    for copy in loads:
        copy.start()

    for half in halves:
        for k in range(tiles):
            for x in (*range(EDGE), *range(size_x + EDGE, size_x + 2 * EDGE)):
                half[x, k, :, :] = jnp.zeros((size_y + 4 * EDGE, LANES), F32)

            @pl.loop(EDGE, size_x + EDGE)
            def _(x, half=half, k=k):
                half[x, k, :low_y, :] = jnp.zeros((low_y, LANES), F32)
                half[x, k, low_y + size_y :, :] = jnp.zeros((low_y, LANES), F32)

    barrier = pltpu.get_barrier_semaphore()
    for _, device in near:
        pl.semaphore_signal(barrier, inc=1, device_id=device, device_id_type=MESH)

    shape = (size_z, size_z)
    apart = jnp.abs(iota(shape, 0) - iota(shape, 1))
    weight = jnp.zeros(shape, F32)
    for k in range(1, 5):
        weight = jnp.where(apart == k, SIDE5[k - 1], weight)
    band[...] = weight.astype(BF16)

    pl.semaphore_wait(barrier, 4)

    def x_copy(half, side):
        turn = int(half is second)
        source = EDGE if side == 0 else size_x
        target = size_x + EDGE if side == 0 else 0
        return pltpu.make_async_remote_copy(
            src_ref=half.at[pl.ds(source, EDGE), :, inner, :],
            dst_ref=half.at[pl.ds(target, EDGE), :, inner, :],
            send_sem=send_sem.at[side],
            recv_sem=recv_sem.at[turn, 1 - side],
            device_id=near[side][1],
            device_id_type=MESH,
        )

    def y_copy(half, side):
        turn = int(half is second)
        return pltpu.make_async_remote_copy(
            src_ref=ysend.at[side],
            dst_ref=yrecv.at[turn, 1 - side],
            send_sem=send_sem.at[2 + side],
            recv_sem=recv_sem.at[turn, 3 - side],
            device_id=near[2 + side][1],
            device_id_type=MESH,
        )

    def send_x(half):
        for side in range(2):

            @pl.when(near[side][0])
            def _(side=side):
                x_copy(half, side).start()

    def send_y(half):
        @pl.loop(0, size_x // 2)
        def _(i):
            for k in range(tiles):
                for j in range(2):
                    at = EDGE + 2 * i + j
                    to = pl.ds(EDGE * j, EDGE)
                    ysend[0, i, k, to, :] = half[at, k, low_y : low_y + EDGE, :]
                    ysend[1, i, k, to, :] = half[at, k, low_y + size_y - EDGE : low_y + size_y, :]

        for side in range(2):

            @pl.when(near[2 + side][0])
            def _(side=side):
                y_copy(half, side).start()

    def wait_x(half):
        for side in range(2):

            @pl.when(near[side][0])
            def _(side=side):
                x_copy(half, side).wait_send()
                x_copy(half, 1 - side).wait_recv()

    def wait_y(half):
        for side in range(2):

            @pl.when(near[2 + side][0])
            def _(side=side):
                y_copy(half, side).wait_send()
                y_copy(half, 1 - side).wait_recv()

                @pl.loop(0, size_x // 2)
                def _(i):
                    for k in range(tiles):
                        for j in range(2):
                            to = low_y - EDGE if side == 0 else low_y + size_y
                            half[EDGE + 2 * i + j, k, to : to + EDGE, :] = yrecv[
                                int(half is second), side, i, k, pl.ds(EDGE * j, EDGE), :
                            ]

    def compute(now, old, t, block):
        base = block * PLANES
        rows_here = PLANES * size_y
        flat = jnp.concatenate(
            [now[pl.ds(EDGE + base, PLANES), k, inner, :].reshape(rows_here, LANES) for k in range(tiles)], axis=1
        )
        top = flat.astype(BF16)
        rest = (flat - top.astype(F32)).astype(BF16)
        part = jnp.dot(top, band[...], preferred_element_type=F32) + jnp.dot(
            rest, band[...], preferred_element_type=F32
        )
        at = pl.multiple_of(base * size_y, rows_here)
        slabs = gath.shape[0]
        left = jnp.concatenate([gath[g, pl.ds(at, rows_here), :] for g in range(slabs)], axis=1)
        source = jnp.dot(left, green[:, t * size_z : (t + 1) * size_z], preferred_element_type=F32)
        for k in range(tiles):
            lanes = slice(k * LANES, (k + 1) * LANES)
            along[:, k] = part[:, lanes].reshape(PLANES, size_y, LANES)
            inject[:, k] = source[:, lanes].reshape(PLANES, size_y, LANES)
        for k in range(tiles):
            for y in range(0, size_y, 8):
                column = [now[base + x, k, pl.ds(low_y + y, 8), :] for x in range(PLANES + 2 * EDGE)]
                for x in range(PLANES):
                    here = column[x + EDGE]
                    lap = CENTER5 * here + along[x, k, pl.ds(y, 8), :]
                    for d in range(1, EDGE + 1):
                        beside = column[x + EDGE + d] + column[x + EDGE - d]
                        beside = beside + now[base + x + EDGE, k, pl.ds(low_y + y + d, 8), :]
                        beside = beside + now[base + x + EDGE, k, pl.ds(low_y + y - d, 8), :]
                        lap = lap + SIDE5[d - 1] * beside
                    spot = (base + x + EDGE, k, pl.ds(low_y + y, 8), slice(None))
                    value = (here + here) - old[spot]
                    value = value + (0.2 * speed[base + x, k, pl.ds(y, 8), :]) * lap
                    old[spot] = value + inject[x, k, pl.ds(y, 8), :]

    for copy in loads[: 2 * tiles]:
        copy.wait()
    send_x(first)
    send_y(first)
    sources = ny
    slabs = gath.shape[0]

    @pl.loop(0, slabs)
    def _(g):
        sum_slab(rows, gath, g, sources)

    for copy in loads[2 * tiles :]:
        copy.wait()

    blocks = size_x // PLANES
    for t in range(STEPS):
        now, old = halves[t % 2], halves[1 - t % 2]
        wait_x(now)
        wait_y(now)

        @pl.loop(0, 2)
        def _(i):
            compute(now, old, t, i * (blocks - 1))

        if t + 1 < STEPS:
            send_x(old)

        @pl.loop(1, blocks - 1)
        def _(i):
            compute(now, old, t, i)

        if t + 1 < STEPS:
            send_y(old)
        if t >= STEPS - 2:
            out = (before_ref, after_ref)[t - STEPS + 2]
            for k in range(tiles):
                pltpu.make_async_copy(
                    old.at[pl.ds(EDGE, size_x), k, inner, :],
                    out.at[:, :, pl.ds(k * LANES, LANES)],
                    store_sem.at[(t - STEPS + 2) * tiles + k],
                ).start()
    for i, out in enumerate((before_ref, after_ref)):
        old = halves[1 - (STEPS - 2 + i) % 2]
        for k in range(tiles):
            pltpu.make_async_copy(
                old.at[pl.ds(EDGE, size_x), k, inner, :],
                out.at[:, :, pl.ds(k * LANES, LANES)],
                store_sem.at[i * tiles + k],
            ).wait()


def on_device(wave_prev, wave_now, courant, traces, pair_owner, pair_cell, green_tiles):
    slab_count, block_count = lax.axis_size("gx"), lax.axis_size("gy")
    owners = slab_count * block_count
    row_count = traces.shape[0]
    size_x, size_y, size_z = wave_now.shape
    tiles = size_z // LANES
    sent = pack(
        pair_owner.reshape(row_count // LANES, LANES),
        pair_cell.reshape(row_count // LANES, LANES),
        traces,
        owners,
    )
    got = lax.all_to_all(sent, ("gx", "gy"), split_axis=0, concat_axis=0, tiled=True)
    any_space = pl.BlockSpec(memory_space=pl.ANY)
    vmem = pl.BlockSpec(memory_space=pltpu.VMEM)
    padded = (size_x + 2 * EDGE, tiles, size_y + 4 * EDGE, LANES)
    face = (2, size_x // 2, tiles, 2 * EDGE, LANES)
    block = (PLANES, tiles, size_y, LANES)
    return pl.pallas_call(
        wave_kernel,
        out_shape=[jax.ShapeDtypeStruct(wave_now.shape, F32)] * 2,
        in_specs=[any_space, any_space, any_space, vmem, any_space],
        out_specs=[any_space, any_space],
        scratch_shapes=[
            pltpu.VMEM(padded, F32),
            pltpu.VMEM(padded, F32),
            pltpu.VMEM((size_x, tiles, size_y, LANES), F32),
            pltpu.VMEM((slab_count, size_x * size_y, LANES), BF16),
            pltpu.VMEM(green_tiles.shape, BF16),
            pltpu.VMEM(block, F32),
            pltpu.VMEM(block, F32),
            pltpu.VMEM((size_z, size_z), BF16),
            pltpu.VMEM(face, F32),
            pltpu.VMEM((2, *face), F32),
            pltpu.SemaphoreType.DMA((3 * tiles + 1,)),
            pltpu.SemaphoreType.DMA((2 * tiles,)),
            pltpu.SemaphoreType.DMA((4,)),
            pltpu.SemaphoreType.DMA((2, 4)),
        ],
        compiler_params=pltpu.CompilerParams(
            vmem_limit_bytes=56 << 20, collective_id=0, has_side_effects=True
        ),
    )(wave_prev, wave_now, courant, got, green_tiles)


def solution(mesh):
    return jax.shard_map(
        on_device,
        mesh=mesh,
        in_specs=(
            P("gx", "gy", None),
            P("gx", "gy", None),
            P("gx", "gy", None),
            P(("gx", "gy"), None),
            P(("gx", "gy"), None),
            P(("gx", "gy")),
            P(("gx", "gy"), None),
        ),
        out_specs=(P("gx", "gy", None), P("gx", "gy", None)),
        check_vma=False,
    )
```

time: 558 us -> 140 us (0.25)
  the two profiles are of different devices: /device:TPU:10 before, /device:TPU:8 now
where the time goes in v1:
time: 140 us
  Pallas kernels  86.8 us (62%)
  blocking collectives  42.5 us (30%)
  local copies, waits for them, and re-layouts  9.73 us (7%)
    pallas_call x1, Pallas kernels, on_device(): pl.pallas_call(wave_kernel, out_shape=[jax.ShapeDtypeStruct(wave_now.shap...  80.1 us
    all_to_all x1, blocking collectives, on_device(): lax.all_to_all(sent, ('gx', 'gy'), split_axis=0, concat_axis=0, tiled=True)  42.5 us
    unnamed x10, local copies, waits for them, and re-layouts  9.73 us
    pallas_call x1, Pallas kernels, pack(): pl.pallas_call(pack_kernel, out_shape=jax.ShapeDtypeStruct((owners, MSG,...  6.74 us

profile of v1, /device:TPU:8, one launch (start us, length us, event | category | flops | bytes accessed | tf_op | source)
XLA Modules:
  0.0 139.7 jit_solution(15719302185206403632)
XLA Ops:
  0.6 0.0 copy-start
  0.6 1.2 copy-done
  1.9 0.0 copy-start.1
  1.9 0.7 copy-done.1
  2.6 0.0 copy-start.2
  2.6 0.7 copy-done.2
  3.3 6.7 %shard_map.86 = bf16[128,72,128]{2,1,0:T(8,128)(2,1)S(1)} custom-call(s32[32,128]{1,0:T(8,128)S(1)} %bitcast.2, s32[32,128]{1,0:T(8,128)S(1)} %bitcast.3, bf16[4096,128]{1,0:T(8,128)(2,1)S(1)} %copy-done), custom_call_target="tpu_custom_call" | custom-call | tf_op jit(solution)/shard_map/pallas_call | solution.py:79
  10.0 42.5 %all_to_all.5.rows = bf16[128,72,128]{2,1,0:T(8,128)(2,1)} all-to-all(bf16[128,72,128]{2,1,0:T(8,128)(2,1)S(1)} %shard_map.86), channel_id=1, replica_groups=mesh['gx'=8,'gy'=16] {'gx','gy'}, dimensions={0} | all-to-all | bytes 4718592 | tf_op jit(solution)/shard_map/all_to_all | solution.py:355
  52.5 80.1 %shard_map.87 = (f32[32,64,512]{2,1,0:T(8,128)}, f32[32,64,512]{2,1,0:T(8,128)}) custom-call(f32[32,64,512]{2,1,0:T(8,128)} %prev_ref.1, f32[32,64,512]{2,1,0:T(8,128)} %now_ref.1, f32[32,64,512]{2,1,0:T(8,128)} %courant_ref.1, bf16[128,72,128]{2,1,0:T(8,128)(2,1)} %all_to_all.5.rows, bf16[1024,2048]{1,0:T(8,128)(2,1)} %green_ref.1), custom_call_target="tpu_custom_call" | custom-call | tf_op jit(solution)/shard_map/pallas_call | solution.py:361
  132.6 0.0 copy-start.3
  132.7 5.1 %copy.11 = f32[32,64,512]{2,1,0:T(8,128)} copy(f32[32,64,512]{2,1,0:T(8,128)} %get-tuple-element.4) | data formatting | bytes 8388608
  137.7 0.0 copy-done.3
  137.7 2.0 %copy.12 = f32[32,64,512]{2,1,0:T(8,128)} copy(f32[32,64,512]{2,1,0:T(8,128)S(1)} %copy-done.3) | data formatting | bytes 8388608
Async XLA Ops:
  0.6 1.2 copy-start
  1.9 0.7 copy-start.1
  2.6 0.7 copy-start.2
  132.6 5.1 %copy-start.3 = (f32[32,64,512]{2,1,0:T(8,128)S(1)}, f32[32,64,512]{2,1,0:T(8,128)}, u32[]{:S(2)}) copy-start(f32[32,64,512]{2,1,0:T(8,128)} %get-tuple-element.5) | copy-start | bytes 12582916

commit v2 on v1

--- a/solution.py
+++ b/solution.py
@@ -14,6 +14,7 @@
 MSG = 72
 EDGE = 4
 PLANES = 4
+THICK = 8
 
 CENTER5 = 3.0 * -205.0 / 72.0 * 5.0
 SIDE5 = (8.0, -1.0, 8.0 / 63.0, -1.0 / 112.0)
@@ -121,14 +122,15 @@
 
 
 def wave_kernel(
-    prev_ref, now_ref, courant_ref, rows, green_ref, before_ref, after_ref,
-    first, second, speed, gath, green, inject, along, band, ysend, yrecv,
-    load_sem, store_sem, send_sem, recv_sem,
+    prev_ref, now_ref, courant_ref, sent, green_ref, before_ref, after_ref,
+    first, second, speed, rows, gath, green, band, ysend, yrecv,
+    load_sem, store_sem, send_sem, recv_sem, row_send_sem, row_recv_sem,
 ):
     gx, gy = lax.axis_index("gx"), lax.axis_index("gy")
     nx, ny = lax.axis_size("gx"), lax.axis_size("gy")
     size_x, size_y, size_z = now_ref.shape
     tiles = size_z // LANES
+    slabs = gath.shape[0]
     halves = (first, second)
     low_y = 2 * EDGE
     inner = pl.ds(low_y, size_y)
@@ -169,9 +171,22 @@
                 half[x, k, :low_y, :] = jnp.zeros((low_y, LANES), F32)
                 half[x, k, low_y + size_y :, :] = jnp.zeros((low_y, LANES), F32)
 
+    def partner(along_x, core, step):
+        chip, mine = gx // 2, lax.rem(gx, 2)
+        there_x = 2 * lax.rem(chip + along_x, nx // 2) + lax.rem(mine + core, 2)
+        inner_step = lax.rem(step, 4)
+        outer_step = lax.rem(step // 4 + step, 4)
+        there_y = 4 * lax.rem(gy // 4 + outer_step, ny // 4) + lax.rem(lax.rem(gy, 4) + inner_step, 4)
+        return there_x, there_y
+
     barrier = pltpu.get_barrier_semaphore()
-    for _, device in near:
-        pl.semaphore_signal(barrier, inc=1, device_id=device, device_id_type=MESH)
+    for along_x in range(nx // 2):
+        for core in range(2):
+
+            @pl.loop(1 if along_x == core == 0 else 0, ny)
+            def _(step, along_x=along_x, core=core):
+                device = partner(along_x, core, step)
+                pl.semaphore_signal(barrier, inc=1, device_id=device, device_id_type=MESH)
 
     shape = (size_z, size_z)
     apart = jnp.abs(iota(shape, 0) - iota(shape, 1))
@@ -180,28 +195,56 @@
         weight = jnp.where(apart == k, SIDE5[k - 1], weight)
     band[...] = weight.astype(BF16)
 
-    pl.semaphore_wait(barrier, 4)
+    pl.semaphore_wait(barrier, nx * ny - 1)
+
+    me = gx * ny + gy
+    keep = pltpu.make_async_copy(sent.at[me], rows.at[me], row_recv_sem.at[gx])
+
+    def send_rows(group):
+        @pl.loop(0, ny)
+        def _(step):
+            for along_x in group:
+                for core in range(2):
+
+                    def send(along_x=along_x, core=core):
+                        there_x, there_y = partner(along_x, core, step)
+                        pltpu.make_async_remote_copy(
+                            src_ref=sent.at[there_x * ny + there_y],
+                            dst_ref=rows.at[me],
+                            send_sem=row_send_sem,
+                            recv_sem=row_recv_sem.at[gx],
+                            device_id=(there_x, there_y),
+                            device_id_type=MESH,
+                        ).start()
+
+                    if along_x == core == 0:
+                        pl.when(step > 0)(send)
+                        pl.when(step == 0)(keep.start)
+                    else:
+                        send()
+
+    def wait_slab(g):
+        part = rows.at[pl.ds(g * ny, ny)]
+        pltpu.make_async_copy(part, part, row_recv_sem.at[g]).wait()
 
     def x_copy(half, side):
-        turn = int(half is second)
         source = EDGE if side == 0 else size_x
         target = size_x + EDGE if side == 0 else 0
         return pltpu.make_async_remote_copy(
             src_ref=half.at[pl.ds(source, EDGE), :, inner, :],
             dst_ref=half.at[pl.ds(target, EDGE), :, inner, :],
             send_sem=send_sem.at[side],
-            recv_sem=recv_sem.at[turn, 1 - side],
+            recv_sem=recv_sem.at[int(half is second), 1 - side],
             device_id=near[side][1],
             device_id_type=MESH,
         )
 
     def y_copy(half, side):
-        turn = int(half is second)
         return pltpu.make_async_remote_copy(
             src_ref=ysend.at[side],
-            dst_ref=yrecv.at[turn, 1 - side],
+            dst_ref=yrecv.at[int(half is second), 1 - side],
             send_sem=send_sem.at[2 + side],
-            recv_sem=recv_sem.at[turn, 3 - side],
+            recv_sem=recv_sem.at[int(half is second), 3 - side],
             device_id=near[2 + side][1],
             device_id_type=MESH,
         )
@@ -254,71 +297,129 @@
                                 int(half is second), side, i, k, pl.ds(EDGE * j, EDGE), :
                             ]
 
-    def compute(now, old, t, block):
-        base = block * PLANES
-        rows_here = PLANES * size_y
-        flat = jnp.concatenate(
-            [now[pl.ds(EDGE + base, PLANES), k, inner, :].reshape(rows_here, LANES) for k in range(tiles)], axis=1
-        )
+    def source_of(t, base):
+        at = pl.multiple_of(base * size_y, THICK * size_y)
+        left = jnp.concatenate([gath[g, pl.ds(at, THICK * size_y), :] for g in range(slabs)], axis=1)
+        return jnp.dot(left, green[:, t * size_z : (t + 1) * size_z], preferred_element_type=F32)
+
+    def local_part(now, old, t, base):
+        count = THICK * size_y
+        place = pl.ds(EDGE + base, THICK)
+        flat = jnp.concatenate([now[place, k, inner, :].reshape(count, LANES) for k in range(tiles)], axis=1)
         top = flat.astype(BF16)
         rest = (flat - top.astype(F32)).astype(BF16)
-        part = jnp.dot(top, band[...], preferred_element_type=F32) + jnp.dot(
-            rest, band[...], preferred_element_type=F32
-        )
-        at = pl.multiple_of(base * size_y, rows_here)
-        slabs = gath.shape[0]
-        left = jnp.concatenate([gath[g, pl.ds(at, rows_here), :] for g in range(slabs)], axis=1)
-        source = jnp.dot(left, green[:, t * size_z : (t + 1) * size_z], preferred_element_type=F32)
+        lap = jnp.dot(top, band[...], preferred_element_type=F32)
+        lap = lap + jnp.dot(rest, band[...], preferred_element_type=F32)
+        source = source_of(t, base) if t else None
         for k in range(tiles):
             lanes = slice(k * LANES, (k + 1) * LANES)
-            along[:, k] = part[:, lanes].reshape(PLANES, size_y, LANES)
-            inject[:, k] = source[:, lanes].reshape(PLANES, size_y, LANES)
+            here = flat[:, lanes]
+            value = (0.2 * speed[pl.ds(base, THICK), k].reshape(count, LANES)) * (CENTER5 * here + lap[:, lanes])
+            value = value + (here + here) - old[place, k, inner, :].reshape(count, LANES)
+            if t:
+                value = value + source[:, lanes]
+            old[place, k, inner, :] = value.reshape(THICK, size_y, LANES)
+
+    def add_source(old, t, base):
+        place = pl.ds(EDGE + base, THICK)
+        source = source_of(t, base)
         for k in range(tiles):
-            for y in range(0, size_y, 8):
+            lanes = source[:, k * LANES : (k + 1) * LANES].reshape(THICK, size_y, LANES)
+            old[place, k, inner, :] = old[place, k, inner, :] + lanes
+
+    def side_part(now, old, base, ys):
+        for k in range(tiles):
+            for y in ys:
                 column = [now[base + x, k, pl.ds(low_y + y, 8), :] for x in range(PLANES + 2 * EDGE)]
                 for x in range(PLANES):
-                    here = column[x + EDGE]
-                    lap = CENTER5 * here + along[x, k, pl.ds(y, 8), :]
+                    lap = None
                     for d in range(1, EDGE + 1):
                         beside = column[x + EDGE + d] + column[x + EDGE - d]
                         beside = beside + now[base + x + EDGE, k, pl.ds(low_y + y + d, 8), :]
                         beside = beside + now[base + x + EDGE, k, pl.ds(low_y + y - d, 8), :]
-                        lap = lap + SIDE5[d - 1] * beside
+                        beside = SIDE5[d - 1] * beside
+                        lap = beside if lap is None else lap + beside
                     spot = (base + x + EDGE, k, pl.ds(low_y + y, 8), slice(None))
-                    value = (here + here) - old[spot]
-                    value = value + (0.2 * speed[base + x, k, pl.ds(y, 8), :]) * lap
-                    old[spot] = value + inject[x, k, pl.ds(y, 8), :]
-
-    for copy in loads[: 2 * tiles]:
+                    old[spot] = old[spot] + (0.2 * speed[base + x, k, pl.ds(y, 8), :]) * lap
+
+    blocks = size_x // PLANES
+    thick_blocks = size_x // THICK
+    every = tuple(range(0, size_y, 8))
+
+    for copy in loads[:tiles]:
         copy.wait()
+    send_rows((0, nx // 4))
     send_x(first)
     send_y(first)
-    sources = ny
-    slabs = gath.shape[0]
-
-    @pl.loop(0, slabs)
-    def _(g):
-        sum_slab(rows, gath, g, sources)
-
-    for copy in loads[2 * tiles :]:
+    send_rows((1, nx // 2 - 1))
+    for copy in loads[tiles : 3 * tiles]:
         copy.wait()
 
-    blocks = size_x // PLANES
-    for t in range(STEPS):
+    @pl.loop(0, thick_blocks)
+    def _(i):
+        local_part(first, second, 0, i * THICK)
+
+    def take_slab(along_x, core):
+        g = 2 * lax.rem(gx // 2 + along_x, nx // 2) + core
+        wait_slab(g)
+        sum_slab(rows, gath, g, ny)
+
+    @pl.loop(0, slabs // 2)
+    def _(i):
+        take_slab(lax.rem(i, 2) * (nx // 4), i // 2)
+
+    wait_x(first)
+    wait_y(first)
+
+    @pl.loop(0, blocks)
+    def _(i):
+        side_part(first, second, i * PLANES, every)
+
+    loads[3 * tiles].wait()
+
+    @pl.loop(0, slabs // 2)
+    def _(i):
+        take_slab(lax.rem(i, 2) * (nx // 4) + 1, i // 2)
+
+    most = rows.at[pl.ds(0, nx * ny - 1)]
+    pltpu.make_async_copy(most, most, row_send_sem).wait()
+
+    @pl.loop(0, 2)
+    def _(i):
+        add_source(second, 0, i * (size_x - THICK))
+
+    send_x(second)
+
+    @pl.loop(1, thick_blocks - 1)
+    def _(i):
+        add_source(second, 0, i * THICK)
+
+    send_y(second)
+
+    for t in range(1, STEPS):
         now, old = halves[t % 2], halves[1 - t % 2]
+
+        @pl.loop(0, thick_blocks)
+        def _(i):
+            local_part(now, old, t, i * THICK)
+
+        @pl.loop(1, blocks - 1)
+        def _(i):
+            side_part(now, old, i * PLANES, every[1:-1])
+
         wait_x(now)
         wait_y(now)
 
         @pl.loop(0, 2)
         def _(i):
-            compute(now, old, t, i * (blocks - 1))
+            side_part(now, old, i * (size_x - PLANES), every)
 
         if t + 1 < STEPS:
             send_x(old)
 
         @pl.loop(1, blocks - 1)
         def _(i):
-            compute(now, old, t, i)
+            side_part(now, old, i * PLANES, (every[0], every[-1]))
 
         if t + 1 < STEPS:
             send_y(old)
@@ -352,25 +453,21 @@
         traces,
         owners,
     )
-    got = lax.all_to_all(sent, ("gx", "gy"), split_axis=0, concat_axis=0, tiled=True)
     any_space = pl.BlockSpec(memory_space=pl.ANY)
-    vmem = pl.BlockSpec(memory_space=pltpu.VMEM)
     padded = (size_x + 2 * EDGE, tiles, size_y + 4 * EDGE, LANES)
     face = (2, size_x // 2, tiles, 2 * EDGE, LANES)
-    block = (PLANES, tiles, size_y, LANES)
     return pl.pallas_call(
         wave_kernel,
         out_shape=[jax.ShapeDtypeStruct(wave_now.shape, F32)] * 2,
-        in_specs=[any_space, any_space, any_space, vmem, any_space],
+        in_specs=[any_space] * 5,
         out_specs=[any_space, any_space],
         scratch_shapes=[
             pltpu.VMEM(padded, F32),
             pltpu.VMEM(padded, F32),
             pltpu.VMEM((size_x, tiles, size_y, LANES), F32),
+            pltpu.VMEM((owners, MSG, LANES), BF16),
             pltpu.VMEM((slab_count, size_x * size_y, LANES), BF16),
             pltpu.VMEM(green_tiles.shape, BF16),
-            pltpu.VMEM(block, F32),
-            pltpu.VMEM(block, F32),
             pltpu.VMEM((size_z, size_z), BF16),
             pltpu.VMEM(face, F32),
             pltpu.VMEM((2, *face), F32),
@@ -378,11 +475,13 @@
             pltpu.SemaphoreType.DMA((2 * tiles,)),
             pltpu.SemaphoreType.DMA((4,)),
             pltpu.SemaphoreType.DMA((2, 4)),
+            pltpu.SemaphoreType.DMA,
+            pltpu.SemaphoreType.DMA((slab_count,)),
         ],
         compiler_params=pltpu.CompilerParams(
             vmem_limit_bytes=56 << 20, collective_id=0, has_side_effects=True
         ),
-    )(wave_prev, wave_now, courant, got, green_tiles)
+    )(wave_prev, wave_now, courant, sent, green_tiles)
 
 
 def solution(mesh):

time: 140 us -> 113 us (0.81)
  blocking collectives: 42.5 us -> 0 us
  Pallas kernels: 86.8 us -> 100 us
    all_to_all x1 -> x0, blocking collectives: 42.5 us -> none  [on_device(): lax.all_to_all(sent, ('gx', 'gy'), split_axis=0, concat_axis=0, tiled=True)]
    pallas_call x1, Pallas kernels: 80.1 us -> 93.7 us  [on_device(): pl.pallas_call(wave_kernel, out_shape=[jax.ShapeDtypeStruct(wave_now.shap...]
    unnamed x10 -> x12, local copies, waits for them, and re-layouts: 9.73 us -> 11.1 us
where the time goes in v2:
time: 113 us; the launch traced here: 112 us
  Pallas kernels  100 us (88%)
  local copies, waits for them, and re-layouts  11.1 us (10%)
    pallas_call x1, Pallas kernels, on_device(): pl.pallas_call(wave_kernel, out_shape=[jax.ShapeDtypeStruct(wave_now.shap...  93.7 us
    unnamed x12, local copies, waits for them, and re-layouts  11.1 us
    pallas_call x1, Pallas kernels, pack(): pl.pallas_call(pack_kernel, out_shape=jax.ShapeDtypeStruct((owners, MSG,...  6.74 us

profile of v2, /device:TPU:8, one launch (start us, length us, event | category | flops | bytes accessed | tf_op | source)
XLA Modules:
  0.0 112.3 jit_solution(15643385330185205843)
XLA Ops:
  0.6 0.0 copy-start.1
  0.6 1.2 %copy-done.1 = bf16[4096,128]{1,0:T(8,128)(2,1)S(1)} copy-done((bf16[4096,128]{1,0:T(8,128)(2,1)S(1)}, bf16[4096,128]{1,0:T(8,128)(2,1)}, u32[]{:S(2)}) %copy-start.1) | copy-done | bytes 1048600
  1.9 0.0 copy-start.2
  1.9 0.7 copy-done.2
  2.6 0.0 copy-start.3
  2.6 0.7 copy-done.3
  3.3 6.7 %shard_map.86.sent = bf16[128,72,128]{2,1,0:T(8,128)(2,1)S(1)} custom-call(s32[32,128]{1,0:T(8,128)S(1)} %bitcast.2, s32[32,128]{1,0:T(8,128)S(1)} %bitcast.3, bf16[4096,128]{1,0:T(8,128)(2,1)S(1)} %copy-done.1), custom_call_target="tpu_custom_call" | custom-call | tf_op jit(solution)/shard_map/pallas_call | solution.py:80
  10.0 0.0 copy-start
  10.1 1.4 %copy-done = bf16[128,72,128]{2,1,0:T(8,128)(2,1)} copy-done((bf16[128,72,128]{2,1,0:T(8,128)(2,1)}, bf16[128,72,128]{2,1,0:T(8,128)(2,1)S(1)}, u32[]{:S(2)}) %copy-start) | copy-done | bytes 2359320
  11.5 93.7 %shard_map.87 = (f32[32,64,512]{2,1,0:T(8,128)}, f32[32,64,512]{2,1,0:T(8,128)}) custom-call(f32[32,64,512]{2,1,0:T(8,128)} %prev_ref.1, f32[32,64,512]{2,1,0:T(8,128)} %now_ref.1, f32[32,64,512]{2,1,0:T(8,128)} %courant_ref.1, bf16[128,72,128]{2,1,0:T(8,128)(2,1)} %copy-done, bf16[1024,2048]{1,0:T(8,128)(2,1)} %green_ref.1), custom_call_target="tpu_custom_call" | custom-call | tf_op jit(solution)/shard_map/pallas_call | solution.py:459
  105.2 0.0 copy-start.4
  105.2 5.1 %copy.11 = f32[32,64,512]{2,1,0:T(8,128)} copy(f32[32,64,512]{2,1,0:T(8,128)} %get-tuple-element.4) | data formatting | bytes 8388608
  110.2 0.0 copy-done.4
  110.2 2.0 %copy.12 = f32[32,64,512]{2,1,0:T(8,128)} copy(f32[32,64,512]{2,1,0:T(8,128)S(1)} %copy-done.4) | data formatting | bytes 8388608
Async XLA Ops:
  0.6 1.2 %copy-start.1 = (bf16[4096,128]{1,0:T(8,128)(2,1)S(1)}, bf16[4096,128]{1,0:T(8,128)(2,1)}, u32[]{:S(2)}) copy-start(bf16[4096,128]{1,0:T(8,128)(2,1)} %trace_ref.1) | copy-start | bytes 3145732
  1.9 0.7 copy-start.2
  2.6 0.7 copy-start.3
  10.0 1.4 %copy-start = (bf16[128,72,128]{2,1,0:T(8,128)(2,1)}, bf16[128,72,128]{2,1,0:T(8,128)(2,1)S(1)}, u32[]{:S(2)}) copy-start(bf16[128,72,128]{2,1,0:T(8,128)(2,1)S(1)} %shard_map.86.sent) | copy-start | bytes 7077892
  105.2 5.1 %copy-start.4 = (f32[32,64,512]{2,1,0:T(8,128)S(1)}, f32[32,64,512]{2,1,0:T(8,128)}, u32[]{:S(2)}) copy-start(f32[32,64,512]{2,1,0:T(8,128)} %get-tuple-element.5) | copy-start | bytes 12582916

commit v3 on v2

--- a/solution.py
+++ b/solution.py
@@ -11,9 +11,8 @@
 BF16 = jnp.bfloat16
 LANES = 128
 SLOTS = 64
-MSG = 72
 EDGE = 4
-PLANES = 4
+PLANES = 2
 THICK = 8
 
 CENTER5 = 3.0 * -205.0 / 72.0 * 5.0
@@ -24,11 +23,24 @@
     return lax.broadcasted_iota(jnp.int32, shape, dim)
 
 
-def pack_kernel(owner_ref, cell_ref, trace_ref, out_ref, wide, rows32, slots_v, slots_s, cells_v, sem):
+def pack_kernel(
+    owner_hbm, cell_hbm, trace_hbm, out_ref, out_cells,
+    owner_ref, cell_ref, trace_ref, wide, rows32, slots_v, slots_s, cells_v, sem, load_sem,
+):
+    loads = [
+        pltpu.make_async_copy(source, target, load_sem.at[i])
+        for i, (source, target) in enumerate(
+            ((owner_hbm, owner_ref), (cell_hbm, cell_ref), (trace_hbm, trace_ref))
+        )
+    ]
+    for load in loads:
+        load.start()
     blocks = owner_ref.shape[0]
     owners = out_ref.shape[0]
     before = (iota((LANES, 2 * LANES), 0) < iota((LANES, 2 * LANES), 1)).astype(F32).astype(BF16)
     carry = jnp.zeros((owners, LANES), F32)
+    loads[0].wait()
+    loads[1].wait()
     cells = jnp.zeros((owners, 2 * SLOTS), F32)
     for i in range(blocks):
         own = owner_ref[i : i + 1, :]
@@ -57,6 +69,7 @@
         at = pl.multiple_of(o * SLOTS, SLOTS)
         wide[pl.ds(at, SLOTS), :] = jnp.zeros((SLOTS, LANES), F32)
 
+    loads[2].wait()
     rows32[...] = trace_ref[...].astype(F32)
     copy.wait()
 
@@ -69,8 +82,8 @@
     @pl.loop(0, owners)
     def _(o):
         at = pl.multiple_of(o * SLOTS, SLOTS)
-        out_ref[o, :SLOTS, :] = wide[pl.ds(at, SLOTS), :].astype(BF16)
-        out_ref[o, SLOTS:, :] = jnp.broadcast_to(cells_v[pl.ds(o, 1), :], (MSG - SLOTS, LANES)).astype(BF16)
+        out_ref[o] = wide[pl.ds(at, SLOTS), :].astype(BF16)
+        out_cells[o] = cells_v[pl.ds(o, 1), :]
 
 
 def pack(owner, cell, traces, owners):
@@ -79,34 +92,41 @@
     vmem = pl.BlockSpec(memory_space=pltpu.VMEM)
     return pl.pallas_call(
         pack_kernel,
-        out_shape=jax.ShapeDtypeStruct((owners, MSG, LANES), BF16),
-        in_specs=[vmem] * 3,
-        out_specs=vmem,
+        out_shape=(
+            jax.ShapeDtypeStruct((owners, SLOTS, LANES), BF16),
+            jax.ShapeDtypeStruct((owners, 1, LANES), F32),
+        ),
+        in_specs=[pl.BlockSpec(memory_space=pltpu.HBM)] * 3,
+        out_specs=(vmem, vmem),
         scratch_shapes=[
+            pltpu.VMEM((blocks, LANES), jnp.int32),
+            pltpu.VMEM((blocks, LANES), jnp.int32),
+            pltpu.VMEM((rows, LANES), BF16),
             pltpu.VMEM((owners * SLOTS, LANES), F32),
             pltpu.VMEM((rows, LANES), F32),
             pltpu.VMEM((blocks, LANES), jnp.int32),
             pltpu.SMEM((blocks, LANES), jnp.int32),
             pltpu.VMEM((owners, 2 * SLOTS), F32),
             pltpu.SemaphoreType.DMA,
+            pltpu.SemaphoreType.DMA((3,)),
         ],
         compiler_params=pltpu.CompilerParams(vmem_limit_bytes=32 << 20),
     )(owner, cell, traces)
 
 
-def sum_slab(rows, gath, g, sources):
+def sum_slab(rows, cells, gath, g, to, sources):
     cell_count = gath.shape[1]
     lane = iota((1, LANES), 1)
     highs, spots, values = [], [], []
     for i in range(0, sources, 2):
-        one = rows[g * sources + i, SLOTS:, :].astype(F32)[:1, :]
-        two = rows[g * sources + i + 1, SLOTS:, :].astype(F32)[:1, :]
+        one = cells[g * sources + i]
+        two = cells[g * sources + i + 1]
         high = jnp.where(lane < SLOTS, one, pltpu.roll(two, SLOTS, 1))
         low = jnp.where(lane < SLOTS, pltpu.roll(one, SLOTS, 1), two)
         highs.append(high)
         spots.append((iota((SLOTS, LANES), 0).astype(F32) == low).astype(F32).astype(BF16))
-        values.append(rows[g * sources + i, :SLOTS, :])
-        values.append(rows[g * sources + i + 1, :SLOTS, :])
+        values.append(rows[g * sources + i])
+        values.append(rows[g * sources + i + 1])
     high = jnp.concatenate(highs, axis=1)
     spot = jnp.concatenate(spots, axis=1)
     value = jnp.concatenate(values, axis=0)
@@ -118,19 +138,19 @@
             picked.append(spot * jnp.broadcast_to(here, spot.shape))
         hot = jnp.concatenate(picked, axis=0)
         total = jnp.dot(hot, value, preferred_element_type=F32)
-        gath[g, first * SLOTS : (first + part) * SLOTS, :] = total.astype(BF16)
+        gath[to, first * SLOTS : (first + part) * SLOTS, :] = total.astype(BF16)
 
 
 def wave_kernel(
-    prev_ref, now_ref, courant_ref, sent, green_ref, before_ref, after_ref,
-    first, second, speed, rows, gath, green, band, ysend, yrecv,
-    load_sem, store_sem, send_sem, recv_sem, row_send_sem, row_recv_sem,
+    prev_ref, now_ref, courant_ref, sent, sent_cells, green_ref, before_ref, after_ref,
+    first, second, speed, rows, cells, gath, green, later, band, ysend, yrecv,
+    load_sem, store_sem, send_sem, recv_sem, row_send_sem, row_recv_sem, cell_send_sem, cell_recv_sem,
 ):
     gx, gy = lax.axis_index("gx"), lax.axis_index("gy")
     nx, ny = lax.axis_size("gx"), lax.axis_size("gy")
     size_x, size_y, size_z = now_ref.shape
     tiles = size_z // LANES
-    slabs = gath.shape[0]
+    groups = gath.shape[0] // 2
     halves = (first, second)
     low_y = 2 * EDGE
     inner = pl.ds(low_y, size_y)
@@ -171,22 +191,33 @@
                 half[x, k, :low_y, :] = jnp.zeros((low_y, LANES), F32)
                 half[x, k, low_y + size_y :, :] = jnp.zeros((low_y, LANES), F32)
 
-    def partner(along_x, core, step):
-        chip, mine = gx // 2, lax.rem(gx, 2)
-        there_x = 2 * lax.rem(chip + along_x, nx // 2) + lax.rem(mine + core, 2)
-        inner_step = lax.rem(step, 4)
-        outer_step = lax.rem(step // 4 + step, 4)
-        there_y = 4 * lax.rem(gy // 4 + outer_step, ny // 4) + lax.rem(lax.rem(gy, 4) + inner_step, 4)
-        return there_x, there_y
+    chips, depth = nx // 2, 4
+
+    def there_x(along, core):
+        return 2 * lax.rem(gx // 2 + along, chips) + lax.rem(gx + core, 2)
+
+    there_zs = [lax.rem(lax.rem(gy, depth) + along, depth) for along in range(depth)]
+
+    def there_y(step, along):
+        return depth * lax.rem(gy // depth + step + along, ny // depth) + there_zs[along]
 
     barrier = pltpu.get_barrier_semaphore()
-    for along_x in range(nx // 2):
-        for core in range(2):
-
-            @pl.loop(1 if along_x == core == 0 else 0, ny)
-            def _(step, along_x=along_x, core=core):
-                device = partner(along_x, core, step)
-                pl.semaphore_signal(barrier, inc=1, device_id=device, device_id_type=MESH)
+
+    @pl.loop(0, ny // depth)
+    def _(step):
+        for along in range(depth):
+            y = there_y(step, along)
+            for along_x in range(chips):
+                for core in range(2):
+                    device = (there_x(along_x, core), y)
+
+                    def greet(device=device):
+                        pl.semaphore_signal(barrier, inc=1, device_id=device, device_id_type=MESH)
+
+                    if along == along_x == core == 0:
+                        pl.when(step > 0)(greet)
+                    else:
+                        greet()
 
     shape = (size_z, size_z)
     apart = jnp.abs(iota(shape, 0) - iota(shape, 1))
@@ -198,34 +229,59 @@
     pl.semaphore_wait(barrier, nx * ny - 1)
 
     me = gx * ny + gy
-    keep = pltpu.make_async_copy(sent.at[me], rows.at[me], row_recv_sem.at[gx])
-
-    def send_rows(group):
-        @pl.loop(0, ny)
+    keep = (
+        pltpu.make_async_copy(sent.at[me], rows.at[me], row_recv_sem.at[gx]),
+        pltpu.make_async_copy(sent_cells.at[me], cells.at[me], cell_recv_sem.at[gx]),
+    )
+
+    def send_rows(first_chip, core):
+        @pl.loop(0, ny // depth)
         def _(step):
-            for along_x in group:
-                for core in range(2):
-
-                    def send(along_x=along_x, core=core):
-                        there_x, there_y = partner(along_x, core, step)
-                        pltpu.make_async_remote_copy(
-                            src_ref=sent.at[there_x * ny + there_y],
-                            dst_ref=rows.at[me],
-                            send_sem=row_send_sem,
-                            recv_sem=row_recv_sem.at[gx],
-                            device_id=(there_x, there_y),
-                            device_id_type=MESH,
-                        ).start()
-
-                    if along_x == core == 0:
+            for along in range(depth):
+                y = there_y(step, along)
+                for along_x in (first_chip, first_chip + chips // 2):
+
+                    def send(x=there_x(along_x, core), y=y):
+                        there = x * ny + y
+                        for source, target, out_sem, in_sem in (
+                            (sent_cells, cells, cell_send_sem, cell_recv_sem),
+                            (sent, rows, row_send_sem, row_recv_sem),
+                        ):
+                            pltpu.make_async_remote_copy(
+                                src_ref=source.at[there],
+                                dst_ref=target.at[me],
+                                send_sem=out_sem,
+                                recv_sem=in_sem.at[gx],
+                                device_id=(x, y),
+                                device_id_type=MESH,
+                            ).start()
+
+                    if along == along_x == 0 and isinstance(core, int) and core == 0:
                         pl.when(step > 0)(send)
-                        pl.when(step == 0)(keep.start)
+
+                        @pl.when(step == 0)
+                        def _():
+                            for copy in keep:
+                                copy.start()
+
                     else:
                         send()
 
-    def wait_slab(g):
-        part = rows.at[pl.ds(g * ny, ny)]
-        pltpu.make_async_copy(part, part, row_recv_sem.at[g]).wait()
+    def slab_of(group, which):
+        chip = lax.rem(gx // 2 + group // 2 + which * (nx // 4), nx // 2)
+        return 2 * chip + lax.rem(gx + group, 2)
+
+    def wait_slabs(group):
+        for which in range(2):
+            g = slab_of(group, which)
+            for target, in_sem in ((cells, cell_recv_sem), (rows, row_recv_sem)):
+                part = target.at[pl.ds(g * ny, ny)]
+                pltpu.make_async_copy(part, part, in_sem.at[g]).wait()
+
+    def sum_slabs(group):
+        @pl.loop(0, 2)
+        def _(which):
+            sum_slab(rows, cells, gath, slab_of(group, which), 2 * group + which, ny)
 
     def x_copy(half, side):
         source = EDGE if side == 0 else size_x
@@ -297,10 +353,17 @@
                                 int(half is second), side, i, k, pl.ds(EDGE * j, EDGE), :
                             ]
 
-    def source_of(t, base):
+    def source_of(half, t, base):
         at = pl.multiple_of(base * size_y, THICK * size_y)
-        left = jnp.concatenate([gath[g, pl.ds(at, THICK * size_y), :] for g in range(slabs)], axis=1)
-        return jnp.dot(left, green[:, t * size_z : (t + 1) * size_z], preferred_element_type=F32)
+        left, right = [], []
+        for group in (2 * half, 2 * half + 1):
+            for which in range(2):
+                left.append(gath[2 * group + which, pl.ds(at, THICK * size_y), :])
+                row = pl.multiple_of(slab_of(group, which) * LANES, LANES)
+                right.append(green[pl.ds(row, LANES), t * size_z : (t + 1) * size_z])
+        return jnp.dot(
+            jnp.concatenate(left, axis=1), jnp.concatenate(right, axis=0), preferred_element_type=F32
+        )
 
     def local_part(now, old, t, base):
         count = THICK * size_y
@@ -310,22 +373,25 @@
         rest = (flat - top.astype(F32)).astype(BF16)
         lap = jnp.dot(top, band[...], preferred_element_type=F32)
         lap = lap + jnp.dot(rest, band[...], preferred_element_type=F32)
-        source = source_of(t, base) if t else None
+        source = source_of(1, t, base) if t else None
         for k in range(tiles):
             lanes = slice(k * LANES, (k + 1) * LANES)
             here = flat[:, lanes]
             value = (0.2 * speed[pl.ds(base, THICK), k].reshape(count, LANES)) * (CENTER5 * here + lap[:, lanes])
             value = value + (here + here) - old[place, k, inner, :].reshape(count, LANES)
             if t:
-                value = value + source[:, lanes]
+                value = value + source[:, lanes] + later[t - 1, pl.ds(base, THICK), k].reshape(count, LANES)
             old[place, k, inner, :] = value.reshape(THICK, size_y, LANES)
 
-    def add_source(old, t, base):
-        place = pl.ds(EDGE + base, THICK)
-        source = source_of(t, base)
+    def add_source(half, t, base):
+        source = source_of(half, t, base)
         for k in range(tiles):
             lanes = source[:, k * LANES : (k + 1) * LANES].reshape(THICK, size_y, LANES)
-            old[place, k, inner, :] = old[place, k, inner, :] + lanes
+            if t:
+                later[t - 1, pl.ds(base, THICK), k] = lanes
+            else:
+                spot = (pl.ds(EDGE + base, THICK), k, inner, slice(None))
+                second[spot] = second[spot] + lanes
 
     def side_part(now, old, base, ys):
         for k in range(tiles):
@@ -344,14 +410,14 @@
 
     blocks = size_x // PLANES
     thick_blocks = size_x // THICK
+    edge_blocks = EDGE // PLANES
     every = tuple(range(0, size_y, 8))
 
+    send_rows(0, 0)
     for copy in loads[:tiles]:
         copy.wait()
-    send_rows((0, nx // 4))
     send_x(first)
     send_y(first)
-    send_rows((1, nx // 2 - 1))
     for copy in loads[tiles : 3 * tiles]:
         copy.wait()
 
@@ -359,15 +425,7 @@
     def _(i):
         local_part(first, second, 0, i * THICK)
 
-    def take_slab(along_x, core):
-        g = 2 * lax.rem(gx // 2 + along_x, nx // 2) + core
-        wait_slab(g)
-        sum_slab(rows, gath, g, ny)
-
-    @pl.loop(0, slabs // 2)
-    def _(i):
-        take_slab(lax.rem(i, 2) * (nx // 4), i // 2)
-
+    send_rows(0, 1)
     wait_x(first)
     wait_y(first)
 
@@ -375,27 +433,36 @@
     def _(i):
         side_part(first, second, i * PLANES, every)
 
+    @pl.loop(0, 2)
+    def _(group):
+        wait_slabs(group)
+        send_rows(1, group)
+        sum_slabs(group)
+
     loads[3 * tiles].wait()
-
-    @pl.loop(0, slabs // 2)
+    for t in range(STEPS):
+
+        @pl.loop(0, thick_blocks)
+        def _(i, t=t):
+            add_source(0, t, i * THICK)
+
+    @pl.loop(2, groups)
+    def _(group):
+        wait_slabs(group)
+        sum_slabs(group)
+
+    for target, out_sem in ((cells, cell_send_sem), (rows, row_send_sem)):
+        most = target.at[pl.ds(0, nx * ny - 1)]
+        pltpu.make_async_copy(most, most, out_sem).wait()
+
+    @pl.loop(0, thick_blocks)
     def _(i):
-        take_slab(lax.rem(i, 2) * (nx // 4) + 1, i // 2)
-
-    most = rows.at[pl.ds(0, nx * ny - 1)]
-    pltpu.make_async_copy(most, most, row_send_sem).wait()
-
-    @pl.loop(0, 2)
-    def _(i):
-        add_source(second, 0, i * (size_x - THICK))
+        add_source(1, 0, i * THICK)
 
     send_x(second)
-
-    @pl.loop(1, thick_blocks - 1)
-    def _(i):
-        add_source(second, 0, i * THICK)
-
     send_y(second)
 
+    stores = []
     for t in range(1, STEPS):
         now, old = halves[t % 2], halves[1 - t % 2]
 
@@ -403,42 +470,44 @@
         def _(i):
             local_part(now, old, t, i * THICK)
 
-        @pl.loop(1, blocks - 1)
+        @pl.loop(edge_blocks, blocks - edge_blocks)
         def _(i):
             side_part(now, old, i * PLANES, every[1:-1])
 
         wait_x(now)
         wait_y(now)
 
-        @pl.loop(0, 2)
+        @pl.loop(0, 2 * edge_blocks)
         def _(i):
-            side_part(now, old, i * (size_x - PLANES), every)
+            block = i + (i // edge_blocks) * (blocks - 2 * edge_blocks)
+            side_part(now, old, block * PLANES, every)
 
         if t + 1 < STEPS:
             send_x(old)
 
-        @pl.loop(1, blocks - 1)
-        def _(i):
-            side_part(now, old, i * PLANES, (every[0], every[-1]))
+        for part in range(2):
+
+            @pl.loop((edge_blocks, blocks // 2)[part], (blocks // 2, blocks - edge_blocks)[part])
+            def _(i):
+                side_part(now, old, i * PLANES, (every[0], every[-1]))
+
+            if t + 2 >= STEPS:
+                out = (before_ref, after_ref)[t + 2 - STEPS]
+                half_x = size_x // 2
+                for k in range(tiles):
+                    stores.append(
+                        pltpu.make_async_copy(
+                            old.at[pl.ds(EDGE + part * half_x, half_x), k, inner, :],
+                            out.at[pl.ds(part * half_x, half_x), :, pl.ds(k * LANES, LANES)],
+                            store_sem.at[len(stores)],
+                        )
+                    )
+                    stores[-1].start()
 
         if t + 1 < STEPS:
             send_y(old)
-        if t >= STEPS - 2:
-            out = (before_ref, after_ref)[t - STEPS + 2]
-            for k in range(tiles):
-                pltpu.make_async_copy(
-                    old.at[pl.ds(EDGE, size_x), k, inner, :],
-                    out.at[:, :, pl.ds(k * LANES, LANES)],
-                    store_sem.at[(t - STEPS + 2) * tiles + k],
-                ).start()
-    for i, out in enumerate((before_ref, after_ref)):
-        old = halves[1 - (STEPS - 2 + i) % 2]
-        for k in range(tiles):
-            pltpu.make_async_copy(
-                old.at[pl.ds(EDGE, size_x), k, inner, :],
-                out.at[:, :, pl.ds(k * LANES, LANES)],
-                store_sem.at[i * tiles + k],
-            ).wait()
+    for copy in stores:
+        copy.wait()
 
 
 def on_device(wave_prev, wave_now, courant, traces, pair_owner, pair_cell, green_tiles):
@@ -447,41 +516,46 @@
     row_count = traces.shape[0]
     size_x, size_y, size_z = wave_now.shape
     tiles = size_z // LANES
-    sent = pack(
+    sent, sent_cells = pack(
         pair_owner.reshape(row_count // LANES, LANES),
         pair_cell.reshape(row_count // LANES, LANES),
         traces,
         owners,
     )
-    any_space = pl.BlockSpec(memory_space=pl.ANY)
+    hbm = pl.BlockSpec(memory_space=pltpu.HBM)
+    vmem = pl.BlockSpec(memory_space=pltpu.VMEM)
     padded = (size_x + 2 * EDGE, tiles, size_y + 4 * EDGE, LANES)
     face = (2, size_x // 2, tiles, 2 * EDGE, LANES)
     return pl.pallas_call(
         wave_kernel,
         out_shape=[jax.ShapeDtypeStruct(wave_now.shape, F32)] * 2,
-        in_specs=[any_space] * 5,
-        out_specs=[any_space, any_space],
+        in_specs=[hbm, hbm, hbm, vmem, vmem, hbm],
+        out_specs=[vmem, hbm],
         scratch_shapes=[
             pltpu.VMEM(padded, F32),
             pltpu.VMEM(padded, F32),
             pltpu.VMEM((size_x, tiles, size_y, LANES), F32),
-            pltpu.VMEM((owners, MSG, LANES), BF16),
+            pltpu.VMEM((owners, SLOTS, LANES), BF16),
+            pltpu.VMEM((owners, 1, LANES), F32),
             pltpu.VMEM((slab_count, size_x * size_y, LANES), BF16),
             pltpu.VMEM(green_tiles.shape, BF16),
+            pltpu.VMEM((STEPS - 1, size_x, tiles, size_y, LANES), F32),
             pltpu.VMEM((size_z, size_z), BF16),
             pltpu.VMEM(face, F32),
             pltpu.VMEM((2, *face), F32),
             pltpu.SemaphoreType.DMA((3 * tiles + 1,)),
-            pltpu.SemaphoreType.DMA((2 * tiles,)),
+            pltpu.SemaphoreType.DMA((4 * tiles,)),
             pltpu.SemaphoreType.DMA((4,)),
             pltpu.SemaphoreType.DMA((2, 4)),
             pltpu.SemaphoreType.DMA,
             pltpu.SemaphoreType.DMA((slab_count,)),
+            pltpu.SemaphoreType.DMA,
+            pltpu.SemaphoreType.DMA((slab_count,)),
         ],
         compiler_params=pltpu.CompilerParams(
-            vmem_limit_bytes=56 << 20, collective_id=0, has_side_effects=True
+            vmem_limit_bytes=43 << 20, collective_id=0, has_side_effects=True
         ),
-    )(wave_prev, wave_now, courant, sent, green_tiles)
+    )(wave_prev, wave_now, courant, sent, sent_cells, green_tiles)
 
 
 def solution(mesh):

time: 113 us -> 99.7 us (0.88)
  Pallas kernels: 100 us -> 91.8 us
  local copies, waits for them, and re-layouts: 11.1 us -> 6.68 us
    pallas_call x1, Pallas kernels: 93.7 us -> 84.9 us  [on_device(): pl.pallas_call(wave_kernel, out_shape=[jax.ShapeDtypeStruct(wave_now.shap...]
    unnamed x12 -> x8, local copies, waits for them, and re-layouts: 11.1 us -> 6.68 us
where the time goes in v3:
time: 99.7 us; the launch traced here: 99.2 us
  Pallas kernels  91.8 us (92%)
  local copies, waits for them, and re-layouts  6.68 us (7%)
    pallas_call x1, Pallas kernels, on_device(): pl.pallas_call(wave_kernel, out_shape=[jax.ShapeDtypeStruct(wave_now.shap...  84.9 us
    pallas_call x1, Pallas kernels, pack(): pl.pallas_call(pack_kernel, out_shape=(jax.ShapeDtypeStruct((owners, SLOT...  6.92 us
    unnamed x8, local copies, waits for them, and re-layouts  6.68 us

profile of v3, /device:TPU:8, one launch (start us, length us, event | category | flops | bytes accessed | tf_op | source)
XLA Modules:
  0.0 99.2 jit_solution(9546077916981656576)
XLA Ops:
  0.6 0.0 copy-start
  0.6 1.2 %copy-done = bf16[4096,128]{1,0:T(8,128)(2,1)S(1)} copy-done((bf16[4096,128]{1,0:T(8,128)(2,1)S(1)}, bf16[4096,128]{1,0:T(8,128)(2,1)}, u32[]{:S(2)}) %copy-start) | copy-done | bytes 1048600
  1.9 0.0 copy-start.1
  1.9 0.7 copy-done.1
  2.6 0.0 copy-start.2
  2.6 0.7 copy-done.2
  3.3 6.9 %shard_map.86 = (bf16[128,64,128]{2,1,0:T(8,128)(2,1)S(1)}, f32[128,1,128]{2,1,0:T(1,128)S(1)}) custom-call(s32[32,128]{1,0:T(8,128)S(1)} %bitcast.2, s32[32,128]{1,0:T(8,128)S(1)} %bitcast.3, bf16[4096,128]{1,0:T(8,128)(2,1)S(1)} %copy-done), custom_call_target="tpu_custom_call" | custom-call | tf_op jit(solution)/shard_map/pallas_call | solution.py:93
  10.2 84.9 %shard_map.87 = (f32[32,64,512]{2,1,0:T(8,128)S(1)}, f32[32,64,512]{2,1,0:T(8,128)S(1)}) custom-call(f32[32,64,512]{2,1,0:T(8,128)} %prev_ref.1, f32[32,64,512]{2,1,0:T(8,128)} %now_ref.1, f32[32,64,512]{2,1,0:T(8,128)} %courant_ref.1, bf16[128,64,128]{2,1,0:T(8,128)(2,1)S(1)} %get-tuple-element.4.sent, f32[128,1,128]{2,1,0:T(1,128)S(1)} %get-tuple-element.5.sent_cells, ...), custom_call_target="tpu_custom_call" | custom-call | tf_op jit(solution)/shard_map/pallas_call | solution.py:529
  95.2 2.0 %copy.11 = f32[32,64,512]{2,1,0:T(8,128)} copy(f32[32,64,512]{2,1,0:T(8,128)S(1)} %get-tuple-element.8) | data formatting | bytes 8388608
  97.2 2.0 %copy.12 = f32[32,64,512]{2,1,0:T(8,128)} copy(f32[32,64,512]{2,1,0:T(8,128)S(1)} %get-tuple-element.9) | data formatting | bytes 8388608
Async XLA Ops:
  0.6 1.2 %copy-start = (bf16[4096,128]{1,0:T(8,128)(2,1)S(1)}, bf16[4096,128]{1,0:T(8,128)(2,1)}, u32[]{:S(2)}) copy-start(bf16[4096,128]{1,0:T(8,128)(2,1)} %trace_hbm.1) | copy-start | bytes 3145732
  1.9 0.7 copy-start.1
  2.6 0.7 copy-start.2

commit v4 on v3

--- a/solution.py
+++ b/solution.py
@@ -150,7 +150,7 @@
     nx, ny = lax.axis_size("gx"), lax.axis_size("gy")
     size_x, size_y, size_z = now_ref.shape
     tiles = size_z // LANES
-    groups = gath.shape[0] // 2
+    slabs = gath.shape[0]
     halves = (first, second)
     low_y = 2 * EDGE
     inner = pl.ds(low_y, size_y)
@@ -160,6 +160,34 @@
         (gy > 0, (gx, lax.rem(gy + ny - 1, ny))),
         (gy < ny - 1, (gx, lax.rem(gy + 1, ny))),
     )
+
+    chips, depth = nx // 2, 4
+
+    def there_x(along, core):
+        return 2 * lax.rem(gx // 2 + along, chips) + lax.rem(gx + core, 2)
+
+    there_zs = [lax.rem(lax.rem(gy, depth) + along, depth) for along in range(depth)]
+
+    def there_y(step, along):
+        return depth * lax.rem(gy // depth + step + along, ny // depth) + there_zs[along]
+
+    barrier = pltpu.get_barrier_semaphore()
+
+    @pl.loop(0, ny // depth)
+    def _(step):
+        for along in range(depth):
+            y = there_y(step, along)
+            for along_x in range(chips):
+                for core in range(2):
+                    device = (there_x(along_x, core), y)
+
+                    def greet(device=device):
+                        pl.semaphore_signal(barrier, inc=1, device_id=device, device_id_type=MESH)
+
+                    if along == along_x == core == 0:
+                        pl.when(step > 0)(greet)
+                    else:
+                        greet()
 
     loads = []
     for i, (source, target) in enumerate(((now_ref, first), (prev_ref, second))):
@@ -181,43 +209,23 @@
     for copy in loads:
         copy.start()
 
-    for half in halves:
-        for k in range(tiles):
-            for x in (*range(EDGE), *range(size_x + EDGE, size_x + 2 * EDGE)):
-                half[x, k, :, :] = jnp.zeros((size_y + 4 * EDGE, LANES), F32)
-
-            @pl.loop(EDGE, size_x + EDGE)
-            def _(x, half=half, k=k):
-                half[x, k, :low_y, :] = jnp.zeros((low_y, LANES), F32)
-                half[x, k, low_y + size_y :, :] = jnp.zeros((low_y, LANES), F32)
-
-    chips, depth = nx // 2, 4
-
-    def there_x(along, core):
-        return 2 * lax.rem(gx // 2 + along, chips) + lax.rem(gx + core, 2)
-
-    there_zs = [lax.rem(lax.rem(gy, depth) + along, depth) for along in range(depth)]
-
-    def there_y(step, along):
-        return depth * lax.rem(gy // depth + step + along, ny // depth) + there_zs[along]
-
-    barrier = pltpu.get_barrier_semaphore()
-
-    @pl.loop(0, ny // depth)
-    def _(step):
-        for along in range(depth):
-            y = there_y(step, along)
-            for along_x in range(chips):
-                for core in range(2):
-                    device = (there_x(along_x, core), y)
-
-                    def greet(device=device):
-                        pl.semaphore_signal(barrier, inc=1, device_id=device, device_id_type=MESH)
-
-                    if along == along_x == core == 0:
-                        pl.when(step > 0)(greet)
-                    else:
-                        greet()
+    for side in range(2):
+        planes = (0, size_x + EDGE)[side]
+        rows_at = (low_y - EDGE, low_y + size_y)[side]
+
+        @pl.when(jnp.logical_not(near[side][0]))
+        def _(planes=planes):
+            for half in halves:
+                for k in range(tiles):
+                    half[planes : planes + EDGE, k, inner, :] = jnp.zeros((EDGE, size_y, LANES), F32)
+
+        @pl.when(jnp.logical_not(near[2 + side][0]))
+        def _(rows_at=rows_at):
+            for half in halves:
+
+                @pl.loop(EDGE, size_x + EDGE)
+                def _(x, half=half):
+                    half[x, :, rows_at : rows_at + EDGE, :] = jnp.zeros((tiles, EDGE, LANES), F32)
 
     shape = (size_z, size_z)
     apart = jnp.abs(iota(shape, 0) - iota(shape, 1))
@@ -234,54 +242,49 @@
         pltpu.make_async_copy(sent_cells.at[me], cells.at[me], cell_recv_sem.at[gx]),
     )
 
-    def send_rows(first_chip, core):
+    def send_rows(along_x, core):
+        own = isinstance(along_x, int) and along_x == core == 0
+
         @pl.loop(0, ny // depth)
         def _(step):
             for along in range(depth):
                 y = there_y(step, along)
-                for along_x in (first_chip, first_chip + chips // 2):
-
-                    def send(x=there_x(along_x, core), y=y):
-                        there = x * ny + y
-                        for source, target, out_sem, in_sem in (
-                            (sent_cells, cells, cell_send_sem, cell_recv_sem),
-                            (sent, rows, row_send_sem, row_recv_sem),
-                        ):
-                            pltpu.make_async_remote_copy(
-                                src_ref=source.at[there],
-                                dst_ref=target.at[me],
-                                send_sem=out_sem,
-                                recv_sem=in_sem.at[gx],
-                                device_id=(x, y),
-                                device_id_type=MESH,
-                            ).start()
-
-                    if along == along_x == 0 and isinstance(core, int) and core == 0:
-                        pl.when(step > 0)(send)
-
-                        @pl.when(step == 0)
-                        def _():
-                            for copy in keep:
-                                copy.start()
-
-                    else:
-                        send()
-
-    def slab_of(group, which):
-        chip = lax.rem(gx // 2 + group // 2 + which * (nx // 4), nx // 2)
-        return 2 * chip + lax.rem(gx + group, 2)
-
-    def wait_slabs(group):
-        for which in range(2):
-            g = slab_of(group, which)
-            for target, in_sem in ((cells, cell_recv_sem), (rows, row_recv_sem)):
-                part = target.at[pl.ds(g * ny, ny)]
-                pltpu.make_async_copy(part, part, in_sem.at[g]).wait()
-
-    def sum_slabs(group):
-        @pl.loop(0, 2)
-        def _(which):
-            sum_slab(rows, cells, gath, slab_of(group, which), 2 * group + which, ny)
+
+                def send(x=there_x(along_x, core), y=y):
+                    there = x * ny + y
+                    for source, target, out_sem, in_sem in (
+                        (sent_cells, cells, cell_send_sem, cell_recv_sem),
+                        (sent, rows, row_send_sem, row_recv_sem),
+                    ):
+                        pltpu.make_async_remote_copy(
+                            src_ref=source.at[there],
+                            dst_ref=target.at[me],
+                            send_sem=out_sem,
+                            recv_sem=in_sem.at[gx],
+                            device_id=(x, y),
+                            device_id_type=MESH,
+                        ).start()
+
+                if along == 0 and own:
+                    pl.when(step > 0)(send)
+
+                    @pl.when(step == 0)
+                    def _():
+                        for copy in keep:
+                            copy.start()
+
+                else:
+                    send()
+
+    def slab_of(turn):
+        chip = lax.rem(gx // 2 + turn // 4 + lax.rem(turn, 2) * (chips // 2), chips)
+        return 2 * chip + lax.rem(gx + turn // 2, 2)
+
+    def wait_slab(turn):
+        g = slab_of(turn)
+        for target, in_sem in ((cells, cell_recv_sem), (rows, row_recv_sem)):
+            part = target.at[pl.ds(g * ny, ny)]
+            pltpu.make_async_copy(part, part, in_sem.at[g]).wait()
 
     def x_copy(half, side):
         source = EDGE if side == 0 else size_x
@@ -356,11 +359,10 @@
     def source_of(half, t, base):
         at = pl.multiple_of(base * size_y, THICK * size_y)
         left, right = [], []
-        for group in (2 * half, 2 * half + 1):
-            for which in range(2):
-                left.append(gath[2 * group + which, pl.ds(at, THICK * size_y), :])
-                row = pl.multiple_of(slab_of(group, which) * LANES, LANES)
-                right.append(green[pl.ds(row, LANES), t * size_z : (t + 1) * size_z])
+        for turn in range(half * slabs // 2, (half + 1) * slabs // 2):
+            left.append(gath[turn, pl.ds(at, THICK * size_y), :])
+            row = pl.multiple_of(slab_of(turn) * LANES, LANES)
+            right.append(green[pl.ds(row, LANES), t * size_z : (t + 1) * size_z])
         return jnp.dot(
             jnp.concatenate(left, axis=1), jnp.concatenate(right, axis=0), preferred_element_type=F32
         )
@@ -377,7 +379,7 @@
         for k in range(tiles):
             lanes = slice(k * LANES, (k + 1) * LANES)
             here = flat[:, lanes]
-            value = (0.2 * speed[pl.ds(base, THICK), k].reshape(count, LANES)) * (CENTER5 * here + lap[:, lanes])
+            value = speed[pl.ds(base, THICK), k].reshape(count, LANES) * (CENTER5 * here + lap[:, lanes])
             value = value + (here + here) - old[place, k, inner, :].reshape(count, LANES)
             if t:
                 value = value + source[:, lanes] + later[t - 1, pl.ds(base, THICK), k].reshape(count, LANES)
@@ -400,13 +402,16 @@
                 for x in range(PLANES):
                     lap = None
                     for d in range(1, EDGE + 1):
-                        beside = column[x + EDGE + d] + column[x + EDGE - d]
-                        beside = beside + now[base + x + EDGE, k, pl.ds(low_y + y + d, 8), :]
+                        beside = now[base + x + EDGE, k, pl.ds(low_y + y + d, 8), :]
                         beside = beside + now[base + x + EDGE, k, pl.ds(low_y + y - d, 8), :]
-                        beside = SIDE5[d - 1] * beside
-                        lap = beside if lap is None else lap + beside
+                        beside = beside + (column[x + EDGE + d] + column[x + EDGE - d])
+                        if SIDE5[d - 1] == -1.0:
+                            lap = lap - beside
+                        else:
+                            beside = SIDE5[d - 1] * beside
+                            lap = beside if lap is None else lap + beside
                     spot = (base + x + EDGE, k, pl.ds(low_y + y, 8), slice(None))
-                    old[spot] = old[spot] + (0.2 * speed[base + x, k, pl.ds(y, 8), :]) * lap
+                    old[spot] = old[spot] + speed[base + x, k, pl.ds(y, 8), :] * lap
 
     blocks = size_x // PLANES
     thick_blocks = size_x // THICK
@@ -414,6 +419,7 @@
     every = tuple(range(0, size_y, 8))
 
     send_rows(0, 0)
+    send_rows(2, 0)
     for copy in loads[:tiles]:
         copy.wait()
     send_x(first)
@@ -421,11 +427,16 @@
     for copy in loads[tiles : 3 * tiles]:
         copy.wait()
 
+    @pl.loop(0, size_x)
+    def _(x):
+        speed[x] = 0.2 * speed[x]
+
     @pl.loop(0, thick_blocks)
     def _(i):
         local_part(first, second, 0, i * THICK)
 
     send_rows(0, 1)
+    send_rows(2, 1)
     wait_x(first)
     wait_y(first)
 
@@ -433,11 +444,11 @@
     def _(i):
         side_part(first, second, i * PLANES, every)
 
-    @pl.loop(0, 2)
-    def _(group):
-        wait_slabs(group)
-        send_rows(1, group)
-        sum_slabs(group)
+    @pl.loop(0, slabs // 2)
+    def _(turn):
+        wait_slab(turn)
+        send_rows(1 + lax.rem(turn, 2) * (chips // 2), turn // 2)
+        sum_slab(rows, cells, gath, slab_of(turn), turn, ny)
 
     loads[3 * tiles].wait()
     for t in range(STEPS):
@@ -446,10 +457,10 @@
         def _(i, t=t):
             add_source(0, t, i * THICK)
 
-    @pl.loop(2, groups)
-    def _(group):
-        wait_slabs(group)
-        sum_slabs(group)
+    @pl.loop(slabs // 2, slabs)
+    def _(turn):
+        wait_slab(turn)
+        sum_slab(rows, cells, gath, slab_of(turn), turn, ny)
 
     for target, out_sem in ((cells, cell_send_sem), (rows, row_send_sem)):
         most = target.at[pl.ds(0, nx * ny - 1)]

time: 99.7 us -> 98 us (0.983)
  Pallas kernels: 91.8 us -> 89.2 us
    pallas_call x1, Pallas kernels: 84.9 us -> 82.3 us  [on_device(): pl.pallas_call(wave_kernel, out_shape=[jax.ShapeDtypeStruct(wave_now.shap...]
where the time goes in v4:
time: 98 us; the launch traced here: 96.6 us
  Pallas kernels  89.2 us (91%)
  local copies, waits for them, and re-layouts  6.68 us (7%)
    pallas_call x1, Pallas kernels, on_device(): pl.pallas_call(wave_kernel, out_shape=[jax.ShapeDtypeStruct(wave_now.shap...  82.3 us
    pallas_call x1, Pallas kernels, pack(): pl.pallas_call(pack_kernel, out_shape=(jax.ShapeDtypeStruct((owners, SLOT...  6.92 us
    unnamed x8, local copies, waits for them, and re-layouts  6.68 us

profile of v4, /device:TPU:8, one launch (start us, length us, event | category | flops | bytes accessed | tf_op | source)
XLA Modules:
  0.0 96.6 jit_solution(11242181016306649766)
XLA Ops:
  0.6 0.0 copy-start
  0.6 1.2 %copy-done = bf16[4096,128]{1,0:T(8,128)(2,1)S(1)} copy-done((bf16[4096,128]{1,0:T(8,128)(2,1)S(1)}, bf16[4096,128]{1,0:T(8,128)(2,1)}, u32[]{:S(2)}) %copy-start) | copy-done | bytes 1048600
  1.9 0.0 copy-start.1
  1.9 0.7 copy-done.1
  2.6 0.0 copy-start.2
  2.6 0.7 copy-done.2
  3.3 6.9 %shard_map.86 = (bf16[128,64,128]{2,1,0:T(8,128)(2,1)S(1)}, f32[128,1,128]{2,1,0:T(1,128)S(1)}) custom-call(s32[32,128]{1,0:T(8,128)S(1)} %bitcast.2, s32[32,128]{1,0:T(8,128)S(1)} %bitcast.3, bf16[4096,128]{1,0:T(8,128)(2,1)S(1)} %copy-done), custom_call_target="tpu_custom_call" | custom-call | tf_op jit(solution)/shard_map/pallas_call | solution.py:93
  10.2 82.3 %shard_map.87 = (f32[32,64,512]{2,1,0:T(8,128)S(1)}, f32[32,64,512]{2,1,0:T(8,128)S(1)}) custom-call(f32[32,64,512]{2,1,0:T(8,128)} %prev_ref.1, f32[32,64,512]{2,1,0:T(8,128)} %now_ref.1, f32[32,64,512]{2,1,0:T(8,128)} %courant_ref.1, bf16[128,64,128]{2,1,0:T(8,128)(2,1)S(1)} %get-tuple-element.4.sent, f32[128,1,128]{2,1,0:T(1,128)S(1)} %get-tuple-element.5.sent_cells, ...), custom_call_target="tpu_custom_call" | custom-call | tf_op jit(solution)/shard_map/pallas_call | solution.py:540
  92.5 2.0 %copy.11 = f32[32,64,512]{2,1,0:T(8,128)} copy(f32[32,64,512]{2,1,0:T(8,128)S(1)} %get-tuple-element.8) | data formatting | bytes 8388608
  94.6 2.0 %copy.12 = f32[32,64,512]{2,1,0:T(8,128)} copy(f32[32,64,512]{2,1,0:T(8,128)S(1)} %get-tuple-element.9) | data formatting | bytes 8388608
Async XLA Ops:
  0.6 1.2 %copy-start = (bf16[4096,128]{1,0:T(8,128)(2,1)S(1)}, bf16[4096,128]{1,0:T(8,128)(2,1)}, u32[]{:S(2)}) copy-start(bf16[4096,128]{1,0:T(8,128)(2,1)} %trace_hbm.1) | copy-start | bytes 3145732
  1.9 0.7 copy-start.1
  2.6 0.7 copy-start.2
